TPU v7x, 32 devices: a whole 2x2x4 slice. The times are simulated.
32 devices in a mesh: draws: 2 (over x), spec: 16 (over z, y, core).
Axes of the slice: x: 2, y: 2, z: 4, core: 2. Of those that a mesh axis runs over, the one named last changes fastest.
Arguments:
- coefficients: bfloat16 [1280, 2, 320, 128], P('draws', None, 'spec'), parts along dimension 0, may hold values from -6 to 6
- legendre: float32 [640, 2, 320, 16], P('spec'), as said below
- row_counts: int32 [16], P('spec'), may hold values from 640 to 1280, as said below
- basis: float32 [64, 128], replicated, may hold values from -0.75 to 0.75
- absorb: float32 [128], replicated, may hold values from 0.00390625 to 0.0625
- peak_level: int32 [512], replicated, may hold values from 0 to 127
- width: float32 [512], replicated, may hold values from 1.5 to 12
Outputs:
- radiance: float32 [32, 2, 1280, 512], P(('draws', 'spec')), parts along dimension 0
There are 2 independent parts, one for each index of `draws`. A program takes and returns all parts, laid end to end along the dimension named above; an argument that names none is the same for every part. Nothing has to cross between parts.
Inputs may be any that keep to these rules, and one draw needn't show every extreme that they name: `legendre`: entry [m, p, s, j] is the associated Legendre function of order m and degree m + 2 s + p, normalised to unit square integral over [-1, 1], at the cosine of a drawn colatitude of row j in the northern hemisphere; it is zero where the degree exceeds 640 - 1. `row_counts`: every count is a multiple of 4; row 0 has 1280 longitudes and row 1 has 640.
All inputs are finite; a program needn't handle non-finite values.
Results may differ from a plain program's by a relative error of at most 0.0003.
Values sent between devices are 32-bit elements; how exact they have to be, the bound alone decides.
A program may use at most 128 MiB of HBM per device.

v0:
```python
import functools
import math

import jax
import jax.numpy as jnp
from jax import lax
from jax.experimental import pallas as pl
from jax.experimental.pallas import tpu as pltpu
from jax.sharding import PartitionSpec as P

NLON = 1280
FINE = 256

PRECISE = lax.Precision.HIGHEST
F32 = jnp.float32
BF16 = jnp.bfloat16


def prior_spread(orders, slots, waves):
    parity = jnp.arange(2, dtype=jnp.int32)[None, :, None]
    degree = orders[:, None, None] + 2 * slots[None, None, :] + parity
    spread = lax.rsqrt((degree + 1).astype(F32) * waves)
    return jnp.where(degree < waves, spread, jnp.zeros_like(spread))


def split(x):
    high = x.astype(BF16)
    return high, (x - high.astype(F32)).astype(BF16)


def dot(a, b):
    return jnp.dot(a, b, preferred_element_type=F32)


def dot3(a, b):
    ah, al = split(a)
    bh, bl = split(b)
    return dot(ah, bh) + dot(al, bh) + dot(ah, bl)


def place_in_ring(n):
    me = lax.axis_index("spec")
    core = me % 2
    side = (me // 2) % 2
    layer = me // 4
    return me, core, side, layer


def exchange_kernel(
    n, draws, waves, coef_hbm, leg_ref, out_ref, coef_ref, send_ref, legs_ref, wide_ref, sums_ref, near_ref, side_ref,
    far_ref, coef_sem, leg_send, leg_recv, pass_send, near_send, near_recv, side_send, side_recv, far_send, far_recv,
):
    me, core, side, layer = place_in_ring(n)
    layers = n // 4
    chunks = n
    chip = me // 2
    draw = lax.axis_index("draws")
    rows = n
    columns = coef_hbm.shape[1]
    every = leg_ref.shape[1]
    slots = every // n
    lanes = 128
    pairs = lanes // rows
    per = pairs // 2
    own = waves // n
    groups = own // per
    depth = per * slots * 2
    part = groups * pairs
    partner = me + 1 - 2 * core
    across = me + 2 - 4 * side

    def spot(z, y, c):
        return (z * 2 + y) * 2 + c

    def remote(src, dst, send_sem, recv_sem, target):
        return pltpu.make_async_remote_copy(
            src_ref=src, dst_ref=dst, send_sem=send_sem, recv_sem=recv_sem,
            device_id={"spec": target}, device_id_type=pl.DeviceIdType.MESH,
        )

    def leg_copy(source, target):
        return remote(send_ref.at[target], legs_ref.at[source], leg_send.at[target], leg_recv.at[source], target)

    def pass_copy(source):
        return pltpu.make_async_remote_copy(
            src_ref=legs_ref.at[source], dst_ref=legs_ref.at[source],
            send_sem=pass_send.at[source], recv_sem=leg_recv.at[source],
            device_id={"draws": 1 - draw}, device_id_type=pl.DeviceIdType.MESH,
        )

    def near_copy(q):
        return remote(sums_ref.at[q, 1 - core], near_ref.at[q], near_send.at[q], near_recv.at[q], partner)

    def side_copy(q):
        return remote(sums_ref.at[q, core, 1 - side], side_ref.at[q], side_send.at[q], side_recv.at[q], across)

    def far_copy(q, source, target):
        return remote(
            sums_ref.at[q, core, side, target], far_ref.at[source, q],
            far_send.at[target, q], far_recv.at[source, q], spot(target, side, core),
        )

    others = [(dz, dy, dc) for dz in range(layers) for dy in range(2) for dc in range(2)][1:]

    def other(offset):
        dz, dy, dc = offset
        return spot((layer + dz) % layers, (side + dy) % 2, (core + dc) % 2)

    coef_copy = pltpu.make_async_copy(coef_hbm, coef_ref, coef_sem)
    coef_copy.start()
    paired = draws == 2
    barrier = pltpu.get_barrier_semaphore()
    if paired:
        pl.semaphore_signal(barrier, inc=1, device_id={"draws": 1 - draw}, device_id_type=pl.DeviceIdType.MESH)
    for offset in others:
        pl.semaphore_signal(barrier, inc=1, device_id={"spec": other(offset)}, device_id_type=pl.DeviceIdType.MESH)

    row = lax.broadcasted_iota(jnp.int32, (lanes, lanes), 0)
    lane = lax.broadcasted_iota(jnp.int32, (lanes, lanes), 1)
    row_at = row % rows
    ordered = ((row_at % 2) * 2 + (row_at // 2) % 2) * layers + row_at // 4
    moves = jnp.where(ordered * pairs + row // rows == lane, 1.0, 0.0)
    leg_row = lax.broadcasted_iota(jnp.int32, (lanes, every), 0) // rows
    leg_slot = lax.broadcasted_iota(jnp.int32, (lanes, every), 1)
    degree_part = leg_row // 2 + leg_row % 2 + 2 * leg_slot

    @pl.loop(0, groups // 2)
    def _(double):
        turned = []
        for half in range(2):
            g = double * 2 + half
            degree = degree_part + (me * own + g * per)
            spread = lax.rsqrt((degree + 1).astype(F32) * float(waves))
            spread = jnp.where(degree < waves, spread, 0.0)
            values = leg_ref[pl.ds(pl.multiple_of(g * lanes, lanes), lanes), :] * spread
            turned.append(
                lax.dot_general(
                    values, moves, (((0,), (0,)), ((), ())), precision=PRECISE, preferred_element_type=F32
                )
            )
        for k in range(n):
            piece = [t[k * slots:(k + 1) * slots] for t in turned]
            send_ref[k, pl.ds(pl.multiple_of(double * 2 * slots, 2 * slots), 2 * slots), :] = jnp.concatenate(piece, 0)

    pl.semaphore_wait(barrier, len(others) + paired)
    sends = (core == draw) if paired else (core >= 0)
    for offset in others:
        target = other(offset)

        @pl.when(jnp.logical_and(sends, me + target < n))
        def _():
            leg_copy(me, target).start()

    legs_ref[me] = send_ref[me]
    coef_copy.wait()

    def receive(owner):
        wanted = jnp.logical_and(owner != me, me + owner < n)
        if not paired:
            return

        @pl.when(jnp.logical_and(wanted, owner % 2 == draw))
        def _():
            leg_copy(owner, me).wait_recv()
            pass_copy(owner).start()

    expand_row = lax.broadcasted_iota(jnp.int32, (depth, lanes), 0)
    expand_lane = lax.broadcasted_iota(jnp.int32, (depth, lanes), 1) % pairs
    keep = (expand_row // (2 * slots)) * 2 + expand_row % 2 == expand_lane

    def partial(q):
        owner = q

        @pl.when(me + owner < n)
        def _():
            waits = owner != me
            if paired:
                waits = jnp.logical_and(waits, owner % 2 != draw)

            @pl.when(waits)
            def _():
                leg_copy(owner, me).wait_recv()

            @pl.loop(0, groups // 2)
            def _(double):
                legs = legs_ref[owner, pl.ds(pl.multiple_of(double * 2 * slots, 2 * slots), 2 * slots), :]
                wide_ref[pl.ds(0, 2 * slots, stride=2), :] = legs
                wide_ref[pl.ds(1, 2 * slots, stride=2), :] = legs
                for half in range(2):
                    g = owner * groups + double * 2 + half
                    values = coef_ref[pl.ds(pl.multiple_of(g * depth, depth), depth), :]
                    one = wide_ref[pl.ds(half * 2 * slots, 2 * slots), :]
                    tiled = jnp.where(keep, jnp.concatenate([one] * per, axis=0), 0.0)
                    both = jnp.concatenate(split(tiled), axis=1)
                    sums = lax.dot_general(both, values, (((0,), (0,)), ((), ())), preferred_element_type=F32)
                    sums = (sums[:lanes] + sums[lanes:]).reshape(2, 2, layers, pairs, columns)
                    at = pl.multiple_of((double * 2 + half) * pairs, pairs)
                    sums_ref[q, :, :, :, pl.ds(at, pairs), :] = sums

        @pl.when(me + owner >= n)
        def _():
            sums_ref[q] = jnp.zeros((2, 2, layers, part, columns), F32)

    def compute(q):
        @pl.when(q + 2 * chip < chunks)
        def _():
            partial(q)
            near_copy(q).start()

    def merge_near(q):
        @pl.when(q + 2 * chip < chunks)
        def _():
            near_copy(q).wait_recv()

            for y in (0, 1):
                @pl.loop(0, layers)
                def _(z):
                    sums_ref[q, core, y, z] += near_ref[q, y, z]

            side_copy(q).start()

    def merge_side(q):
        here = q + 2 * chip < chunks
        there = q + 2 * (across // 2) < chunks

        @pl.when(there)
        def _():
            side_copy(q).wait_recv()

        @pl.when(jnp.logical_and(here, there))
        def _():
            @pl.loop(0, layers)
            def _(z):
                sums_ref[q, core, side, z] += side_ref[q, z]

        @pl.when(jnp.logical_and(jnp.logical_not(here), there))
        def _():
            @pl.loop(0, layers)
            def _(z):
                sums_ref[q, core, side, z] = side_ref[q, z]

        @pl.when(jnp.logical_or(here, there))
        def _():
            for dz in range(1, layers):
                far_copy(q, layer, (layer + dz) % layers).start()

    lag = min(5, chunks)
    ahead = 2
    for owner in range(ahead):
        receive(owner)

    @pl.loop(0, chunks + 1)
    def _(t):
        @pl.when(t + ahead < chunks)
        def _():
            receive(t + ahead)

        @pl.when(t < chunks)
        def _():
            compute(t)

        @pl.when(t >= 1)
        def _():
            merge_near(t - 1)

        @pl.when(t >= lag)
        def _():
            merge_side(t - lag)

    @pl.loop(chunks + 1 - lag, chunks)
    def _(q):
        merge_side(q)

    @pl.loop(0, chunks)
    def _(q):
        at = pl.ds(pl.multiple_of(q * part, part), part)

        @pl.when(q + 4 * layer < chunks)
        def _():
            out_ref[at, :] = sums_ref[q, core, side, layer]

        @pl.when(q + 4 * layer >= chunks)
        def _():
            out_ref[at, :] = jnp.zeros((part, columns), F32)

        for dz in range(1, layers):
            source = (layer + dz) % layers

            @pl.when(q + 4 * source < chunks)
            def _():
                far_copy(q, source, layer).wait_recv()
                out_ref[at, :] += far_ref[source, q]

    for offset in others:
        target = other(offset)

        @pl.when(jnp.logical_and(sends, me + target < n))
        def _():
            leg_copy(me, target).wait_send()

    if paired:
        @pl.loop(0, n)
        def _(owner):
            @pl.when(jnp.logical_and(owner != me, jnp.logical_and(me + owner < n, owner % 2 == draw)))
            def _():
                pass_copy(owner).wait_send()

    @pl.loop(0, chunks)
    def _(q):
        @pl.when(q + 2 * chip < chunks)
        def _():
            near_copy(q).wait_send()
            side_copy(q).wait_send()

        @pl.when(q + 4 * layer < chunks)
        def _():
            for dz in range(1, layers):
                far_copy(q, layer, (layer + dz) % layers).wait_send()


def exchanged_sums(coefficients, legendre, n, draws):
    waves, _, slots, columns = coefficients.shape
    own, _, every, rows = legendre.shape
    dense = jnp.transpose(coefficients, (0, 2, 1, 3)).reshape(waves * slots * 2, columns)
    legs = jnp.transpose(legendre, (0, 1, 3, 2)).reshape(own * 2 * rows, every)
    layers, chunks = n // 4, n
    pairs = 128 // rows
    groups = own * 2 // pairs
    width = groups * pairs
    dma = pltpu.SemaphoreType.DMA

    def body(*refs):
        exchange_kernel(n, draws, waves, *refs)

    return pl.pallas_call(
        body,
        out_shape=jax.ShapeDtypeStruct((2 * waves, columns), F32),
        in_specs=[pl.BlockSpec(memory_space=pl.ANY), pl.BlockSpec(memory_space=pltpu.VMEM)],
        out_specs=pl.BlockSpec(memory_space=pltpu.VMEM),
        scratch_shapes=[
            pltpu.VMEM(dense.shape, BF16),
            pltpu.VMEM((n, groups * slots, 128), F32),
            pltpu.VMEM((n, groups * slots, 128), F32),
            pltpu.VMEM((4 * slots, 128), F32),
            pltpu.VMEM((chunks, 2, 2, layers, width, columns), F32),
            pltpu.VMEM((chunks, 2, layers, width, columns), F32),
            pltpu.VMEM((chunks, layers, width, columns), F32),
            pltpu.VMEM((layers, chunks, width, columns), F32),
            dma, dma((n,)), dma((n,)), dma((n,)),
            dma((chunks,)), dma((chunks,)),
            dma((chunks,)), dma((chunks,)),
            dma((layers, chunks)), dma((layers, chunks)),
        ],
        compiler_params=pltpu.CompilerParams(
            collective_id=0, has_side_effects=True, vmem_limit_bytes=58 * 1024 * 1024
        ),
        name="exchanged_sums",
    )(dense, legs)


def row_kernel(
    count_ref, spectra_ref, basis_ref, absorb_ref, peak_ref, width_ref, out_ref,
    fcos_ref, fsin_ref, ccos_ref, csin_ref, high_ref, low_ref, rhigh_ref, rlow_ref,
):
    step = pl.program_id(0)
    waves = fcos_ref.shape[1]
    levels = absorb_ref.shape[1]
    points = fcos_ref.shape[0]
    tiny = 16
    middle = points // tiny

    @pl.when(step == 0)
    def _():
        count = count_ref[0].astype(F32)
        table = (tiny + middle + ccos_ref.shape[0], waves)
        index = lax.broadcasted_iota(jnp.int32, table, 0)
        order = lax.broadcasted_iota(jnp.int32, table, 1)
        places = jnp.where(index < tiny, index, (index - tiny) * tiny)
        places = jnp.where(index < tiny + middle, places, (index - tiny - middle) * points)
        phases = (places * order).astype(F32)
        phases = phases - jnp.floor(phases / count) * count
        angles = 2.0 * math.pi * phases / count
        cosine, sine = jnp.cos(angles), jnp.sin(angles)
        weights = jnp.where(order == 0, 1.0, 2.0) * jnp.where(2 * order < count_ref[0], 1.0, 0.0)
        first = tiny + middle
        ccos_ref[...] = (cosine * weights)[first:]
        csin_ref[...] = (sine * weights)[first:]
        for b in range(middle):
            turn_c, turn_s = cosine[tiny + b:tiny + b + 1], sine[tiny + b:tiny + b + 1]
            fcos_ref[pl.ds(b * tiny, tiny), :] = cosine[:tiny] * turn_c - sine[:tiny] * turn_s
            fsin_ref[pl.ds(b * tiny, tiny), :] = sine[:tiny] * turn_c + cosine[:tiny] * turn_s

        even = spectra_ref[pl.ds(0, waves, stride=2), :]
        odd = spectra_ref[pl.ds(1, waves, stride=2), :]
        half = even.shape[1] // 2
        real = jnp.concatenate((even[:, :half], odd[:, :half]), axis=1)
        imag = jnp.concatenate((even[:, half:], odd[:, half:]), axis=1)
        basis = basis_ref[...]
        top = jnp.concatenate((basis, basis), axis=1)
        wide = jnp.concatenate((top, jnp.concatenate((basis, -basis), axis=1)), axis=0)
        for index, piece in enumerate((real, imag)):
            high, low = split(dot3(piece, wide))
            high_ref[pl.ds(index * waves, waves), :] = high
            low_ref[pl.ds(index * waves, waves), :] = low
        height = lax.broadcasted_iota(jnp.int32, rlow_ref.shape, 0)
        offsets = (height - peak_ref[...]).astype(F32) / width_ref[...]
        shape = jnp.exp(-offsets * offsets)
        high, low = split(shape / jnp.sum(shape, axis=0, keepdims=True))
        rhigh_ref[pl.ds(0, levels), :] = high
        rhigh_ref[pl.ds(levels, levels), :] = high
        rlow_ref[...] = low

    base_c = ccos_ref[pl.ds(step, 1), :]
    base_s = csin_ref[pl.ds(step, 1), :]
    fine_c = fcos_ref[...]
    fine_s = fsin_ref[...]
    cosine = base_c * fine_c - base_s * fine_s
    sine = -(base_s * fine_c + base_c * fine_s)
    lookup_high, lookup_low = split(jnp.concatenate((cosine, sine), axis=1))
    temps = dot(jnp.concatenate((lookup_high, lookup_low), axis=0), high_ref[...])
    temps = temps[:points] + temps[points:] + dot(lookup_high, low_ref[...])
    temps = jnp.concatenate((temps[:, :levels], temps[:, levels:]), axis=0)

    source = jnp.exp(0.5 * temps)
    layers = absorb_ref[...] * source
    before = lax.broadcasted_iota(jnp.int32, (2 * levels, levels), 0) % levels
    after = lax.broadcasted_iota(jnp.int32, (2 * levels, levels), 1)
    upper = jnp.where(before < after, 1.0, 0.0).astype(BF16)
    layers_high, layers_low = split(layers)
    above = dot(jnp.concatenate((layers_high, layers_low), axis=1), upper)
    emitted = source * jnp.exp(-above) * (1.0 - jnp.exp(-layers))
    place = step * points + lax.broadcasted_iota(jnp.int32, (2 * points, levels), 0) % points
    emitted = jnp.where(place < count_ref[0], emitted, 0.0)
    emitted_high, emitted_low = split(emitted)
    bright = dot(jnp.concatenate((emitted_high, emitted_low), axis=1), rhigh_ref[...])
    bright = bright + dot(emitted_high, rlow_ref[...])
    out_ref[0, 0] = bright[:points]
    out_ref[0, 1] = bright[points:]


def synthesize_row(spectra, row_counts, basis, absorb, peak_level, width, points):
    waves = spectra.shape[0] // 2
    levels, channels = absorb.shape[0], width.shape[0]
    columns = spectra.shape[1]
    steps = points // FINE
    coarse = -(-steps // 8) * 8

    def whole(*shape):
        return pl.BlockSpec(shape, lambda i, *_: (0,) * len(shape))

    return pl.pallas_call(
        row_kernel,
        out_shape=jax.ShapeDtypeStruct((1, 2, points, channels), F32),
        grid_spec=pltpu.PrefetchScalarGridSpec(
            num_scalar_prefetch=1,
            grid=(steps,),
            in_specs=[
                whole(2 * waves, columns),
                whole(*basis.shape),
                whole(1, levels),
                whole(1, channels),
                whole(1, channels),
            ],
            out_specs=pl.BlockSpec((1, 2, FINE, channels), lambda i, *_: (0, 0, i, 0)),
            scratch_shapes=[
                pltpu.VMEM((FINE, waves), F32),
                pltpu.VMEM((FINE, waves), F32),
                pltpu.VMEM((coarse, waves), F32),
                pltpu.VMEM((coarse, waves), F32),
                pltpu.VMEM((2 * waves, 2 * levels), BF16),
                pltpu.VMEM((2 * waves, 2 * levels), BF16),
                pltpu.VMEM((2 * levels, channels), BF16),
                pltpu.VMEM((levels, channels), BF16),
            ],
        ),
        name="row_synthesis",
    )(row_counts, spectra, basis, absorb[None, :], peak_level[None, :], width[None, :])


def moved_coefficients(coefficients, legendre):
    waves, _, slots, _ = coefficients.shape
    first = lax.axis_index("spec") * slots
    spread = prior_spread(jnp.arange(waves, dtype=jnp.int32), first + jnp.arange(slots, dtype=jnp.int32), waves)
    scaled = coefficients.astype(F32) * spread[..., None]
    spectral = lax.all_to_all(scaled, "spec", split_axis=0, concat_axis=2, tiled=True)
    sums = jnp.einsum("mpsj,mpsc->mpjc", legendre, spectral, precision=PRECISE)
    sums = lax.all_to_all(sums, "spec", split_axis=2, concat_axis=0, tiled=True)
    return sums.reshape(2 * waves, sums.shape[-1])


def on_device(draws, coefficients, legendre, row_counts, basis, absorb, peak_level, width):
    own, _, every, rows = legendre.shape
    waves, _, slots, columns = coefficients.shape
    n = waves // own
    fits = n == rows and n % 8 == 0 and 128 % n == 0 and every == n * slots and columns == 128
    fits = fits and (128 // n) % 8 == 0 and own % (128 // n) == 0 and slots % 4 == 0
    if fits and (slots * 128 // n) % 16 == 0 and 2 * waves >= 2 * slots * n:
        spectra = exchanged_sums(coefficients, legendre, n, draws)
    else:
        spectra = moved_coefficients(coefficients, legendre)
    return synthesize_row(spectra, row_counts, basis, absorb, peak_level, width, NLON)


def solution(mesh):
    placed = (
        P("draws", None, "spec", None),
        P("spec", None, None, None),
        P("spec"),
        P(),
        P(),
        P(),
        P(),
    )
    return jax.shard_map(
        functools.partial(on_device, mesh.shape["draws"]),
        mesh=mesh,
        in_specs=placed,
        out_specs=P(("draws", "spec"), None, None, None),
        check_vma=False,
    )
```

profile of v0, /device:TPU:12, one launch (start us, length us, event | category | flops | bytes accessed | tf_op | source)
XLA Modules:
  0.0 95.2 jit_solution(9779804255894694126)
XLA Ops:
  0.7 82.0 %exchanged_sums.1.spectra_ref = f32[1280,128]{1,0:T(8,128)} custom-call(bf16[25600,128]{1,0:T(8,128)(2,1)} %bitcast.9, f32[1280,320]{1,0:T(8,128)} %bitcast.10), custom_call_target="tpu_custom_call" | custom-call | tf_op jit(solution)/shard_map/exchanged_sums/pallas_call | solution.py:335
  82.7 12.5 %row_synthesis.1 = f32[1,2,1280,512]{3,2,1,0:T(8,128)} custom-call(s32[1]{0:T(128)S(6)} %copy.8.count_ref, f32[1280,128]{1,0:T(8,128)} %exchanged_sums.1.spectra_ref, f32[64,128]{1,0:T(8,128)} %basis_ref.1, f32[1,128]{1,0:T(1,128)} %bitcast.13, s32[1,512]{1,0:T(1,128)} %bitcast.11, f32[1,512]{1,0:T(1,128)} %bitcast.12), custom_call_target="tpu_custom_call" | custom-call | tf_op jit(solution)/shard_map/row_synthesis/pallas_call | solution.py:451
where the time goes:
time: 96.6 us; the launch traced here: 95.2 us
  Pallas kernels  94.5 us (98%)
    pallas_call x1, Pallas kernels, exchanged_sums(): pl.pallas_call(body, out_shape=jax.ShapeDtypeStruct((2 * waves, columns),...  82 us
    pallas_call x1, Pallas kernels, synthesize_row(): pl.pallas_call(row_kernel, out_shape=jax.ShapeDtypeStruct((1, 2, points,...  12.5 us

commit v1 on v0

v1 whole, which is shorter than its diff:
```python
import math

import jax
import jax.numpy as jnp
from jax import lax
from jax.experimental import pallas as pl
from jax.experimental.pallas import tpu as pltpu
from jax.sharding import PartitionSpec as P

NLON = 1280
FINE = 256
LANES = 128

PRECISE = lax.Precision.HIGHEST
F32 = jnp.float32
BF16 = jnp.bfloat16


def prior_spread(orders, slots, waves):
    parity = jnp.arange(2, dtype=jnp.int32)[None, :, None]
    degree = orders[:, None, None] + 2 * slots[None, None, :] + parity
    spread = lax.rsqrt((degree + 1).astype(F32) * waves)
    return jnp.where(degree < waves, spread, jnp.zeros_like(spread))


def split(x):
    high = x.astype(BF16)
    return high, (x - high.astype(F32)).astype(BF16)


def dot(a, b):
    return jnp.dot(a, b, preferred_element_type=F32)


def dot3(a, b):
    ah, al = split(a)
    bh, bl = split(b)
    return dot(ah, bh) + dot(al, bh) + dot(ah, bl)


def place_in_ring(n):
    me = lax.axis_index("spec")
    core = me % 2
    side = (me // 2) % 2
    layer = me // 4
    return me, core, side, layer


def trig_tile(tile, count, spectra_ref, basis_ref, fcos_ref, fsin_ref, temps_ref):
    points, lanes = fcos_ref.shape
    steps = temps_ref.shape[0] // points
    tiny = 16
    middle = points // tiny
    coarse = -(-steps // 8) * 8
    whole = count.astype(F32)
    table = (tiny + middle + coarse, lanes)
    index = lax.broadcasted_iota(jnp.int32, table, 0)
    order = lax.broadcasted_iota(jnp.int32, table, 1) + tile * lanes
    places = jnp.where(index < tiny, index, (index - tiny) * tiny)
    places = jnp.where(index < tiny + middle, places, (index - tiny - middle) * points)
    phases = (places * order).astype(F32)
    phases = phases - jnp.floor(phases / whole) * whole
    angles = 2.0 * math.pi * phases / whole
    cosine, sine = jnp.cos(angles), jnp.sin(angles)
    weights = jnp.where(order == 0, 1.0, 2.0) * jnp.where(2 * order < count, 1.0, 0.0)
    first = tiny + middle
    base_c, base_s = (cosine * weights)[first:], (sine * weights)[first:]
    for b in range(middle):
        turn_c, turn_s = cosine[tiny + b:tiny + b + 1], sine[tiny + b:tiny + b + 1]
        fcos_ref[pl.ds(b * tiny, tiny), :] = cosine[:tiny] * turn_c - sine[:tiny] * turn_s
        fsin_ref[pl.ds(b * tiny, tiny), :] = sine[:tiny] * turn_c + cosine[:tiny] * turn_s

    even = spectra_ref[pl.ds(2 * lanes * tile, lanes, stride=2), :]
    odd = spectra_ref[pl.ds(2 * lanes * tile + 1, lanes, stride=2), :]
    half = even.shape[1] // 2
    real = jnp.concatenate((even[:, :half], odd[:, :half]), axis=1)
    imag = jnp.concatenate((even[:, half:], odd[:, half:]), axis=1)
    basis = basis_ref[...]
    top = jnp.concatenate((basis, basis), axis=1)
    wide = jnp.concatenate((top, jnp.concatenate((basis, -basis), axis=1)), axis=0)
    high, low = split(dot3(jnp.concatenate((real, imag), axis=0), wide))
    fine_c, fine_s = fcos_ref[...], fsin_ref[...]
    for step in range(steps):
        turn_c, turn_s = base_c[step:step + 1], base_s[step:step + 1]
        lookup_c = turn_c * fine_c - turn_s * fine_s
        lookup_s = -(turn_s * fine_c + turn_c * fine_s)
        lookup_high, lookup_low = split(jnp.concatenate((lookup_c, lookup_s), axis=1))
        temps = dot(jnp.concatenate((lookup_high, lookup_low), axis=0), high)
        temps = temps[:points] + temps[points:] + dot(lookup_high, low)
        at = pl.ds(step * points, points)
        if tile == 0:
            temps_ref[at, :] = temps
        else:
            temps_ref[at, :] += temps


def exchange_kernel(
    n, waves, count_ref, coef_hbm, leg_ref, basis_ref, temps_ref, coef_ref, turn_ref, raw_ref, send_ref, seed_ref,
    wide_ref, sums_ref, near_ref, side_ref, far_ref, spectra_ref, fcos_ref, fsin_ref, coef_sem, seed_send, seed_recv,
    near_send, near_recv, side_send, side_recv, far_send, far_recv, diag_send,
):
    me, core, side, layer = place_in_ring(n)
    layers = n // 4
    chunks = n
    chip = me // 2
    rows = n
    columns = coef_hbm.shape[1]
    every = leg_ref.shape[1]
    slots = every // n
    lanes = LANES
    pairs = lanes // rows
    per = pairs // 2
    own = waves // n
    groups = own // per
    depth = per * slots * 2
    part = groups * pairs
    room = seed_ref.shape[1] // 2
    partner = me + 1 - 2 * core
    across = me + 2 - 4 * side

    def spot(z, y, c):
        return (z * 2 + y) * 2 + c

    def remote(src, dst, send_sem, recv_sem, target):
        return pltpu.make_async_remote_copy(
            src_ref=src, dst_ref=dst, send_sem=send_sem, recv_sem=recv_sem,
            device_id={"spec": target}, device_id_type=pl.DeviceIdType.MESH,
        )

    def seed_copy(source, target):
        return remote(send_ref.at[target], seed_ref.at[source], seed_send.at[target], seed_recv.at[source], target)

    def near_copy(q):
        return remote(sums_ref.at[q, 1 - core], near_ref.at[q], near_send.at[q], near_recv.at[q], partner)

    def side_copy(q, z):
        return remote(
            sums_ref.at[q, core, 1 - side, z], side_ref.at[q, z], side_send.at[q, z], side_recv.at[q, z], across
        )

    def far_copy(q, source, target):
        return remote(
            sums_ref.at[q, core, side, target], far_ref.at[source, q],
            far_send.at[target, q], far_recv.at[source, q], spot(target, side, core),
        )

    def diag_copy(q, target):
        return remote(
            sums_ref.at[q, core, 1 - side, target], far_ref.at[layer, q],
            diag_send.at[target, q], far_recv.at[layer, q], spot(target, 1 - side, core),
        )

    def signal(target):
        pl.semaphore_signal(barrier, inc=1, device_id={"spec": target}, device_id_type=pl.DeviceIdType.MESH)

    corners = [(dy, dc) for dy in range(2) for dc in range(2)]

    def corner(z, offset):
        dy, dc = offset
        return spot(z, (side + dy) % 2, (core + dc) % 2)

    coef_copy = pltpu.make_async_copy(coef_hbm, coef_ref, coef_sem)
    coef_copy.start()
    barrier = pltpu.get_barrier_semaphore()
    for offset in corners[1:]:
        signal(corner(layer, offset))

    @pl.when(layer > 0)
    def _():
        for dz in range(1, layers - 1):
            for offset in corners:
                signal(corner(1 + (layer - 1 + dz) % (layers - 1), offset))

    row = lax.broadcasted_iota(jnp.int32, (lanes, lanes), 0)
    lane = lax.broadcasted_iota(jnp.int32, (lanes, lanes), 1)
    row_at = row % rows
    ordered = ((row_at % 2) * 2 + (row_at // 2) % 2) * layers + row_at // 4
    moves = jnp.where(ordered * pairs + row // rows == lane, 1.0, 0.0).astype(BF16)

    raw_ref[...] = jnp.zeros(raw_ref.shape, F32)
    for g in range(groups):
        turn_ref[...] = jnp.transpose(leg_ref[pl.ds(g * lanes, lanes), :])
        raw_ref[pl.ds(g, n, stride=2 * room), :] = turn_ref[pl.ds(0, n, stride=slots), :]
        raw_ref[pl.ds(room + g, n, stride=2 * room), :] = turn_ref[pl.ds(1, n, stride=slots), :]
    start = jnp.broadcast_to(raw_ref[pl.ds(0, 1), :], (8, lanes))
    cosine = pltpu.roll(start, lanes - rows, 1) / start
    sine = pltpu.roll(start, lanes - 2 * rows, 1) / start
    sine = sine * sine * (2.0 / 3.0)
    square = jnp.where(sine < 0.5, 1.0 - sine, cosine * cosine * (1.0 / 3.0))
    square = jnp.where(lax.broadcasted_iota(jnp.int32, (8, lanes), 1) < rows, square, 0.0)
    shift = rows
    while shift < lanes:
        square = square + pltpu.roll(square, shift, 1)
        shift *= 2
    square = jnp.where(me == 0, square, 0.0)
    raw_ref[pl.ds(groups, n, stride=2 * room), :] = jnp.broadcast_to(square[:1], (n, lanes))
    raw = raw_ref[...]
    high = raw.astype(BF16)
    rest = raw - high.astype(F32)
    middle = rest.astype(BF16)
    low = (rest - middle.astype(F32)).astype(BF16)
    send_ref[...] = (dot(high, moves) + (dot(middle, moves) + dot(low, moves))).reshape(send_ref.shape)
    seed_ref[me] = send_ref[me]

    def give_seeds(z, offset):
        target = corner(z, offset)

        @pl.when(me + target < n)
        def _():
            seed_copy(me, target).start()

    @pl.when(layer == 0)
    def _():
        pl.semaphore_wait(barrier, len(corners) - 1)
        for dz in range(1, layers):
            for offset in corners:
                signal(corner(dz, offset))
        for offset in corners[1:]:
            give_seeds(layer, offset)

    @pl.when(layer > 0)
    def _():
        pl.semaphore_wait(barrier, n - 1)
        for offset in corners:
            signal(corner(0, offset))
        for offset in corners[1:]:
            give_seeds(layer, offset)
        for dz in range(1, layers):
            for offset in corners:
                give_seeds((layer + dz) % layers, offset)

    def meet():
        @pl.when(layer == 0)
        def _():
            pl.semaphore_wait(barrier, n - len(corners))
            for dz in range(1, layers):
                for offset in corners:
                    give_seeds(dz, offset)

    coef_copy.wait()

    expand_row = lax.broadcasted_iota(jnp.int32, (depth, lanes), 0)
    expand_lane = lax.broadcasted_iota(jnp.int32, (depth, lanes), 1) % pairs
    keep = (expand_row // (2 * slots)) * 2 + expand_row % 2 == expand_lane
    pair_at = lax.broadcasted_iota(jnp.int32, (room, lanes), 1) % pairs
    order_part = lax.broadcasted_iota(jnp.int32, (room, lanes), 0) * per + pair_at // 2

    def recur(owner):
        order = order_part + owner * own
        first = order + pair_at % 2 + me * (2 * slots)
        m = order.astype(F32)
        square = seed_ref[0, pl.ds(groups, 1), :]

        def coupling(d):
            return ((d - m) * (d + m)) / ((2.0 * d - 1.0) * (2.0 * d + 1.0))

        def place(s, value):
            degree = first + 2 * s
            spread = lax.rsqrt((degree + 1).astype(F32) * float(waves))
            value = value * jnp.where(degree < waves, spread, 0.0)
            wide_ref[pl.ds(2 * s, room, stride=2 * slots), :] = value
            wide_ref[pl.ds(2 * s + 1, room, stride=2 * slots), :] = value

        before = seed_ref[owner, pl.ds(0, room), :]
        now = seed_ref[owner, pl.ds(room, room), :]
        place(0, before)
        place(1, now)
        degree = first.astype(F32)
        last = coupling(degree + 2.0)
        weight = jnp.sqrt(coupling(degree + 1.0) * last)
        for s in range(1, slots - 1):
            degree = degree + 2.0
            one, two = coupling(degree + 1.0), coupling(degree + 2.0)
            product = one * two
            inverse = lax.rsqrt(product)
            before, now = now, ((square - (one + last)) * now - weight * before) * inverse
            weight = product * inverse
            last = two
            place(s + 1, now)

    def partial(owner):
        @pl.when(me + owner < n)
        def _():
            @pl.when(owner != me)
            def _():
                seed_copy(owner, me).wait_recv()

            recur(owner)

            @pl.loop(0, groups // 2)
            def _(double):
                for half in range(2):
                    g = double * 2 + half
                    at = owner * groups + g
                    values = coef_ref[pl.ds(pl.multiple_of(at * depth, depth), depth), :]
                    one = wide_ref[pl.ds(pl.multiple_of(g * 2 * slots, 2 * slots), 2 * slots), :]
                    tiled = jnp.where(keep, jnp.concatenate([one] * per, axis=0), 0.0)
                    both = jnp.concatenate(split(tiled), axis=1)
                    sums = lax.dot_general(both, values, (((0,), (0,)), ((), ())), preferred_element_type=F32)
                    sums = (sums[:lanes] + sums[lanes:]).reshape(2, 2, layers, pairs, columns)
                    sums_ref[owner, :, :, :, pl.ds(pl.multiple_of(g * pairs, pairs), pairs), :] = sums

        @pl.when(me + owner >= n)
        def _():
            sums_ref[owner] = jnp.zeros((2, 2, layers, part, columns), F32)

    def held(q, place):
        return q + 2 * place < chunks

    def compute(q):
        @pl.when(held(q, chip))
        def _():
            partial(q)
            near_copy(q).start()

    def merge_near(q):
        shared = jnp.logical_and(held(q, chip), held(q, across // 2))
        alone = jnp.logical_and(held(q, chip), jnp.logical_not(held(q, across // 2)))

        @pl.when(held(q, chip))
        def _():
            near_copy(q).wait_recv()

            for y in (0, 1):
                @pl.loop(0, layers)
                def _(z):
                    sums_ref[q, core, y, z] += near_ref[q, y, z]

        @pl.when(shared)
        def _():
            for dz in range(1, layers):
                side_copy(q, (layer + dz) % layers).start()

        @pl.when(alone)
        def _():
            for dz in range(1, layers):
                far_copy(q, layer, (layer + dz) % layers).start()
                diag_copy(q, (layer + dz) % layers).start()

    def merge_side(q):
        @pl.when(jnp.logical_and(held(q, chip), held(q, across // 2)))
        def _():
            for dz in range(1, layers):
                z = (layer + dz) % layers
                side_copy(q, z).wait_recv()
                sums_ref[q, core, side, z] += side_ref[q, z]
                far_copy(q, layer, z).start()

    lag = 3

    @pl.loop(0, chunks + lag)
    def _(t):
        @pl.when(t < chunks)
        def _():
            compute(t)

        @pl.when(t == 1)
        def _():
            meet()

        @pl.when(jnp.logical_and(t >= 1, t <= chunks))
        def _():
            merge_near(t - 1)

        @pl.when(t == chunks)
        def _():
            @pl.loop(0, chunks)
            def _(q):
                @pl.when(held(q, chip))
                def _():
                    side_copy(q, layer).start()

        @pl.when(t >= lag)
        def _():
            merge_side(t - lag)

    def finish(q):
        at = pl.ds(pl.multiple_of(q * part, part), part)

        @pl.when(held(q, chip))
        def _():
            spectra_ref[at, :] = sums_ref[q, core, side, layer]

        @pl.when(jnp.logical_not(held(q, chip)))
        def _():
            spectra_ref[at, :] = jnp.zeros((part, columns), F32)

        for dz in range(1, layers):
            source = (layer + dz) % layers

            @pl.when(q + 4 * source < chunks)
            def _():
                far_copy(q, source, layer).wait_recv()
                spectra_ref[at, :] += far_ref[source, q]

        @pl.when(held(q, across // 2))
        def _():
            side_copy(q, layer).wait_recv()
            spectra_ref[at, :] += side_ref[q, layer]

    tiles = waves // lanes
    done = 0
    for tile in range(tiles):
        until = -(-(tile + 1) * lanes // own)

        @pl.loop(done, until)
        def _(q):
            finish(q)

        done = until
        trig_tile(tile, count_ref[0], spectra_ref, basis_ref, fcos_ref, fsin_ref, temps_ref)

    @pl.loop(0, n)
    def _(target):
        @pl.when(jnp.logical_and(target != me, me + target < n))
        def _():
            seed_copy(me, target).wait_send()

    @pl.loop(0, chunks)
    def _(q):
        @pl.when(held(q, chip))
        def _():
            near_copy(q).wait_send()
            side_copy(q, layer).wait_send()
            for dz in range(1, layers):
                z = (layer + dz) % layers
                far_copy(q, layer, z).wait_send()

                @pl.when(held(q, across // 2))
                def _():
                    side_copy(q, z).wait_send()

                @pl.when(jnp.logical_not(held(q, across // 2)))
                def _():
                    diag_copy(q, z).wait_send()


def exchanged_temps(coefficients, legendre, row_counts, basis, n, points):
    waves, _, slots, columns = coefficients.shape
    own, _, every, rows = legendre.shape
    dense = jnp.transpose(coefficients, (0, 2, 1, 3)).reshape(waves * slots * 2, columns)
    legs = jnp.transpose(legendre, (0, 1, 3, 2)).reshape(own * 2 * rows, every)
    layers, chunks = n // 4, n
    pairs = LANES // rows
    groups = own * 2 // pairs
    width = groups * pairs
    room = -(-(groups + 1) // 8) * 8
    dma = pltpu.SemaphoreType.DMA

    def body(*refs):
        exchange_kernel(n, waves, *refs)

    vmem = pl.BlockSpec(memory_space=pltpu.VMEM)
    return pl.pallas_call(
        body,
        out_shape=jax.ShapeDtypeStruct((points, 2 * basis.shape[1]), F32),
        in_specs=[pl.BlockSpec(memory_space=pltpu.SMEM), pl.BlockSpec(memory_space=pl.ANY), vmem, vmem],
        out_specs=vmem,
        scratch_shapes=[
            pltpu.VMEM(dense.shape, BF16),
            pltpu.VMEM((every, LANES), F32),
            pltpu.VMEM((n * 2 * room, LANES), F32),
            pltpu.VMEM((n, 2 * room, LANES), F32),
            pltpu.VMEM((n, 2 * room, LANES), F32),
            pltpu.VMEM((room * 2 * slots, LANES), F32),
            pltpu.VMEM((chunks, 2, 2, layers, width, columns), F32),
            pltpu.VMEM((chunks, 2, layers, width, columns), F32),
            pltpu.VMEM((chunks, layers, width, columns), F32),
            pltpu.VMEM((layers, chunks, width, columns), F32),
            pltpu.VMEM((2 * waves, columns), F32),
            pltpu.VMEM((FINE, LANES), F32),
            pltpu.VMEM((FINE, LANES), F32),
            dma, dma((n,)), dma((n,)),
            dma((chunks,)), dma((chunks,)),
            dma((chunks, layers)), dma((chunks, layers)),
            dma((layers, chunks)), dma((layers, chunks)), dma((layers, chunks)),
        ],
        compiler_params=pltpu.CompilerParams(
            collective_id=0, has_side_effects=True, vmem_limit_bytes=58 * 1024 * 1024
        ),
        name="exchanged_temps",
    )(row_counts, dense, legs, basis)


def plain_temps(spectra, row_counts, basis, points):
    tiles = spectra.shape[0] // (2 * LANES)

    def body(count_ref, spectra_ref, basis_ref, temps_ref, fcos_ref, fsin_ref):
        for tile in range(tiles):
            trig_tile(tile, count_ref[0], spectra_ref, basis_ref, fcos_ref, fsin_ref, temps_ref)

    vmem = pl.BlockSpec(memory_space=pltpu.VMEM)
    return pl.pallas_call(
        body,
        out_shape=jax.ShapeDtypeStruct((points, 2 * basis.shape[1]), F32),
        in_specs=[pl.BlockSpec(memory_space=pltpu.SMEM), vmem, vmem],
        out_specs=vmem,
        scratch_shapes=[pltpu.VMEM((FINE, LANES), F32), pltpu.VMEM((FINE, LANES), F32)],
        name="plain_temps",
    )(row_counts, spectra, basis)


def row_kernel(count_ref, temps_ref, absorb_ref, peak_ref, width_ref, out_ref, rhigh_ref, rlow_ref):
    step = pl.program_id(0)
    levels = absorb_ref.shape[1]
    points = temps_ref.shape[0]

    @pl.when(step == 0)
    def _():
        height = lax.broadcasted_iota(jnp.int32, rlow_ref.shape, 0)
        offsets = (height - peak_ref[...]).astype(F32) / width_ref[...]
        shape = jnp.exp(-offsets * offsets)
        high, low = split(shape / jnp.sum(shape, axis=0, keepdims=True))
        rhigh_ref[pl.ds(0, levels), :] = high
        rhigh_ref[pl.ds(levels, levels), :] = high
        rlow_ref[...] = low

    temps = temps_ref[...]
    temps = jnp.concatenate((temps[:, :levels], temps[:, levels:]), axis=0)

    source = jnp.exp(0.5 * temps)
    layers = absorb_ref[...] * source
    before = lax.broadcasted_iota(jnp.int32, (2 * levels, levels), 0) % levels
    after = lax.broadcasted_iota(jnp.int32, (2 * levels, levels), 1)
    upper = jnp.where(before < after, 1.0, 0.0).astype(BF16)
    layers_high, layers_low = split(layers)
    above = dot(jnp.concatenate((layers_high, layers_low), axis=1), upper)
    emitted = source * jnp.exp(-above) * (1.0 - jnp.exp(-layers))
    place = step * points + lax.broadcasted_iota(jnp.int32, (2 * points, levels), 0) % points
    emitted = jnp.where(place < count_ref[0], emitted, 0.0)
    emitted_high, emitted_low = split(emitted)
    bright = dot(jnp.concatenate((emitted_high, emitted_low), axis=1), rhigh_ref[...])
    bright = bright + dot(emitted_high, rlow_ref[...])
    out_ref[0, 0] = bright[:points]
    out_ref[0, 1] = bright[points:]


def radiate_row(temps, row_counts, absorb, peak_level, width):
    points = temps.shape[0]
    levels, channels = absorb.shape[0], width.shape[0]

    def whole(*shape):
        return pl.BlockSpec(shape, lambda i, *_: (0,) * len(shape))

    return pl.pallas_call(
        row_kernel,
        out_shape=jax.ShapeDtypeStruct((1, 2, points, channels), F32),
        grid_spec=pltpu.PrefetchScalarGridSpec(
            num_scalar_prefetch=1,
            grid=(points // FINE,),
            in_specs=[
                pl.BlockSpec((FINE, 2 * levels), lambda i, *_: (i, 0)),
                whole(1, levels),
                whole(1, channels),
                whole(1, channels),
            ],
            out_specs=pl.BlockSpec((1, 2, FINE, channels), lambda i, *_: (0, 0, i, 0)),
            scratch_shapes=[
                pltpu.VMEM((2 * levels, channels), BF16),
                pltpu.VMEM((levels, channels), BF16),
            ],
        ),
        name="row_radiance",
    )(row_counts, temps, absorb[None, :], peak_level[None, :], width[None, :])


def moved_coefficients(coefficients, legendre):
    waves, _, slots, _ = coefficients.shape
    first = lax.axis_index("spec") * slots
    spread = prior_spread(jnp.arange(waves, dtype=jnp.int32), first + jnp.arange(slots, dtype=jnp.int32), waves)
    scaled = coefficients.astype(F32) * spread[..., None]
    spectral = lax.all_to_all(scaled, "spec", split_axis=0, concat_axis=2, tiled=True)
    sums = jnp.einsum("mpsj,mpsc->mpjc", legendre, spectral, precision=PRECISE)
    sums = lax.all_to_all(sums, "spec", split_axis=2, concat_axis=0, tiled=True)
    return sums.reshape(2 * waves, sums.shape[-1])


def on_device(coefficients, legendre, row_counts, basis, absorb, peak_level, width):
    own, _, every, rows = legendre.shape
    waves, _, slots, columns = coefficients.shape
    n = waves // own
    fits = n == rows and n % 8 == 0 and LANES % n == 0 and every == n * slots and columns == LANES
    fits = fits and (LANES // n) % 8 == 0 and own % (LANES // n) == 0 and slots % 4 == 0 and waves % LANES == 0
    if fits and (slots * LANES // n) % 16 == 0 and 2 * waves >= 2 * slots * n:
        temps = exchanged_temps(coefficients, legendre, row_counts, basis, n, NLON)
    else:
        spectra = moved_coefficients(coefficients, legendre)
        temps = plain_temps(spectra, row_counts, basis, NLON)
    return radiate_row(temps, row_counts, absorb, peak_level, width)


def solution(mesh):
    placed = (
        P("draws", None, "spec", None),
        P("spec", None, None, None),
        P("spec"),
        P(),
        P(),
        P(),
        P(),
    )
    return jax.shard_map(
        on_device,
        mesh=mesh,
        in_specs=placed,
        out_specs=P(("draws", "spec"), None, None, None),
        check_vma=False,
    )
```

time: 96.6 us -> 88.4 us (0.915)
  the two profiles are of different devices: /device:TPU:12 before, /device:TPU:26 now
where the time goes in v1:
time: 88.4 us; the launch traced here: 88.1 us
  Pallas kernels  87.5 us (99%)
    pallas_call x1, Pallas kernels, exchanged_temps(): pl.pallas_call(body, out_shape=jax.ShapeDtypeStruct((points, 2 * basis.sh...  80.9 us
    pallas_call x1, Pallas kernels, radiate_row(): pl.pallas_call(row_kernel, out_shape=jax.ShapeDtypeStruct((1, 2, points,...  6.54 us

profile of v1, /device:TPU:26, one launch (start us, length us, event | category | flops | bytes accessed | tf_op | source)
XLA Modules:
  0.0 88.1 jit_solution(2020379847292506711)
XLA Ops:
  0.7 80.9 %exchanged_temps.1.temps_ref = f32[1280,256]{1,0:T(8,128)} custom-call(s32[1]{0:T(128)S(6)} %copy.8.refs_0_.count_ref, bf16[25600,128]{1,0:T(8,128)(2,1)} %bitcast.9, f32[1280,320]{1,0:T(8,128)} %bitcast.10, f32[64,128]{1,0:T(8,128)} %refs_3_.1), custom_call_target="tpu_custom_call" | custom-call | tf_op jit(solution)/shard_map/exchanged_temps/pallas_call | solution.py:454
  81.6 6.5 %row_radiance.1 = f32[1,2,1280,512]{3,2,1,0:T(8,128)} custom-call(s32[1]{0:T(128)S(6)} %copy.8.refs_0_.count_ref, f32[1280,256]{1,0:T(8,128)} %exchanged_temps.1.temps_ref, f32[1,128]{1,0:T(1,128)} %bitcast.13, s32[1,512]{1,0:T(1,128)} %bitcast.11, f32[1,512]{1,0:T(1,128)} %bitcast.12), custom_call_target="tpu_custom_call" | custom-call | tf_op jit(solution)/shard_map/row_radiance/pallas_call | solution.py:545

commit v2 on v1

--- a/solution.py
+++ b/solution.py
@@ -96,8 +96,8 @@
 
 def exchange_kernel(
     n, waves, count_ref, coef_hbm, leg_ref, basis_ref, temps_ref, coef_ref, turn_ref, raw_ref, send_ref, seed_ref,
-    wide_ref, sums_ref, near_ref, side_ref, far_ref, spectra_ref, fcos_ref, fsin_ref, coef_sem, seed_send, seed_recv,
-    near_send, near_recv, side_send, side_recv, far_send, far_recv, diag_send,
+    wide_ref, sums_ref, near_ref, side_ref, far_ref, up_ref, spectra_ref, fcos_ref, fsin_ref, coef_sem, seed_send, seed_recv,
+    near_send, near_recv, side_send, side_recv, far_send, far_recv, up_recv, diag_send,
 ):
     me, core, side, layer = place_in_ring(n)
     layers = n // 4
@@ -142,6 +142,12 @@
         return remote(
             sums_ref.at[q, core, side, target], far_ref.at[source, q],
             far_send.at[target, q], far_recv.at[source, q], spot(target, side, core),
+        )
+
+    def up_copy(q, target):
+        return remote(
+            sums_ref.at[q, core, side, target], up_ref.at[q, target],
+            far_send.at[target, q], up_recv.at[q, target], spot((layer + 1) % layers, side, core),
         )
 
     def diag_copy(q, target):
@@ -315,7 +321,6 @@
 
     def merge_near(q):
         shared = jnp.logical_and(held(q, chip), held(q, across // 2))
-        alone = jnp.logical_and(held(q, chip), jnp.logical_not(held(q, across // 2)))
 
         @pl.when(held(q, chip))
         def _():
@@ -328,23 +333,39 @@
 
         @pl.when(shared)
         def _():
-            for dz in range(1, layers):
+            for dz in reversed(range(1, layers)):
                 side_copy(q, (layer + dz) % layers).start()
 
-        @pl.when(alone)
-        def _():
-            for dz in range(1, layers):
-                far_copy(q, layer, (layer + dz) % layers).start()
-                diag_copy(q, (layer + dz) % layers).start()
-
-    def merge_side(q):
-        @pl.when(jnp.logical_and(held(q, chip), held(q, across // 2)))
-        def _():
-            for dz in range(1, layers):
+    def pass_on(q):
+        shared = held(q, across // 2)
+
+        @pl.when(held(q, chip))
+        def _():
+            for dz in reversed(range(1, layers)):
                 z = (layer + dz) % layers
-                side_copy(q, z).wait_recv()
-                sums_ref[q, core, side, z] += side_ref[q, z]
-                far_copy(q, layer, z).start()
+                upward = jnp.logical_and(z > layer + 1, held(q, chip + 2))
+
+                @pl.when(shared)
+                def _():
+                    side_copy(q, z).wait_recv()
+                    sums_ref[q, core, side, z] += side_ref[q, z]
+
+                @pl.when(jnp.logical_and(layer > 0, z > layer))
+                def _():
+                    up_copy(q, z).wait_recv()
+                    sums_ref[q, core, side, z] += up_ref[q, z]
+
+                @pl.when(upward)
+                def _():
+                    up_copy(q, z).start()
+
+                @pl.when(jnp.logical_not(upward))
+                def _():
+                    far_copy(q, layer, z).start()
+
+                @pl.when(jnp.logical_not(shared))
+                def _():
+                    diag_copy(q, z).start()
 
     lag = 3
 
@@ -362,7 +383,7 @@
         def _():
             merge_near(t - 1)
 
-        @pl.when(t == chunks)
+        @pl.when(t == chunks - 2 * chip)
         def _():
             @pl.loop(0, chunks)
             def _(q):
@@ -372,7 +393,7 @@
 
         @pl.when(t >= lag)
         def _():
-            merge_side(t - lag)
+            pass_on(t - lag)
 
     def finish(q):
         at = pl.ds(pl.multiple_of(q * part, part), part)
@@ -388,7 +409,9 @@
         for dz in range(1, layers):
             source = (layer + dz) % layers
 
-            @pl.when(q + 4 * source < chunks)
+            passed = jnp.logical_and(source + 1 < layer, held(q, 2 * (source + 1) + side))
+
+            @pl.when(jnp.logical_and(held(q, 2 * source), jnp.logical_not(passed)))
             def _():
                 far_copy(q, source, layer).wait_recv()
                 spectra_ref[at, :] += far_ref[source, q]
@@ -467,13 +490,14 @@
             pltpu.VMEM((chunks, 2, layers, width, columns), F32),
             pltpu.VMEM((chunks, layers, width, columns), F32),
             pltpu.VMEM((layers, chunks, width, columns), F32),
+            pltpu.VMEM((chunks, layers, width, columns), F32),
             pltpu.VMEM((2 * waves, columns), F32),
             pltpu.VMEM((FINE, LANES), F32),
             pltpu.VMEM((FINE, LANES), F32),
             dma, dma((n,)), dma((n,)),
             dma((chunks,)), dma((chunks,)),
             dma((chunks, layers)), dma((chunks, layers)),
-            dma((layers, chunks)), dma((layers, chunks)), dma((layers, chunks)),
+            dma((layers, chunks)), dma((layers, chunks)), dma((chunks, layers)), dma((layers, chunks)),
         ],
         compiler_params=pltpu.CompilerParams(
             collective_id=0, has_side_effects=True, vmem_limit_bytes=58 * 1024 * 1024

time: 88.4 us -> 81.4 us (0.921)
  the two profiles are of different devices: /device:TPU:26 before, /device:TPU:5 now
where the time goes in v2:
time: 81.4 us; the launch traced here: 81.2 us
  Pallas kernels  80.5 us (99%)
    pallas_call x1, Pallas kernels, exchanged_temps(): pl.pallas_call(body, out_shape=jax.ShapeDtypeStruct((points, 2 * basis.sh...  74 us
    pallas_call x1, Pallas kernels, radiate_row(): pl.pallas_call(row_kernel, out_shape=jax.ShapeDtypeStruct((1, 2, points,...  6.54 us

profile of v2, /device:TPU:5, one launch (start us, length us, event | category | flops | bytes accessed | tf_op | source)
XLA Modules:
  0.0 81.2 jit_solution(13882080537659023074)
XLA Ops:
  0.7 74.0 %exchanged_temps.1.temps_ref = f32[1280,256]{1,0:T(8,128)} custom-call(s32[1]{0:T(128)S(6)} %copy.8.refs_0_.count_ref, bf16[25600,128]{1,0:T(8,128)(2,1)} %bitcast.9, f32[1280,320]{1,0:T(8,128)} %bitcast.10, f32[64,128]{1,0:T(8,128)} %refs_3_.1), custom_call_target="tpu_custom_call" | custom-call | tf_op jit(solution)/shard_map/exchanged_temps/pallas_call | solution.py:477
  74.6 6.5 %row_radiance.1 = f32[1,2,1280,512]{3,2,1,0:T(8,128)} custom-call(s32[1]{0:T(128)S(6)} %copy.8.refs_0_.count_ref, f32[1280,256]{1,0:T(8,128)} %exchanged_temps.1.temps_ref, f32[1,128]{1,0:T(1,128)} %bitcast.13, s32[1,512]{1,0:T(1,128)} %bitcast.11, f32[1,512]{1,0:T(1,128)} %bitcast.12), custom_call_target="tpu_custom_call" | custom-call | tf_op jit(solution)/shard_map/row_radiance/pallas_call | solution.py:569

commit v3 on v2

--- a/solution.py
+++ b/solution.py
@@ -46,9 +46,9 @@
     return me, core, side, layer
 
 
-def trig_tile(tile, count, spectra_ref, basis_ref, fcos_ref, fsin_ref, temps_ref):
+def fill_lookup(tile, count, fcos_ref, fsin_ref, high_ref, low_ref):
     points, lanes = fcos_ref.shape
-    steps = temps_ref.shape[0] // points
+    steps = high_ref.shape[0] // points
     tiny = 16
     middle = points // tiny
     coarse = -(-steps // 8) * 8
@@ -69,7 +69,18 @@
         turn_c, turn_s = cosine[tiny + b:tiny + b + 1], sine[tiny + b:tiny + b + 1]
         fcos_ref[pl.ds(b * tiny, tiny), :] = cosine[:tiny] * turn_c - sine[:tiny] * turn_s
         fsin_ref[pl.ds(b * tiny, tiny), :] = sine[:tiny] * turn_c + cosine[:tiny] * turn_s
-
+    fine_c, fine_s = fcos_ref[...], fsin_ref[...]
+    for step in range(steps):
+        turn_c, turn_s = base_c[step:step + 1], base_s[step:step + 1]
+        lookup_c = turn_c * fine_c - turn_s * fine_s
+        lookup_s = -(turn_s * fine_c + turn_c * fine_s)
+        high, low = split(jnp.concatenate((lookup_c, lookup_s), axis=1))
+        high_ref[pl.ds(step * points, points), :] = high
+        low_ref[pl.ds(step * points, points), :] = low
+
+
+def add_tile(tile, spectra_ref, basis_ref, high_ref, low_ref, temps_ref):
+    lanes = LANES
     even = spectra_ref[pl.ds(2 * lanes * tile, lanes, stride=2), :]
     odd = spectra_ref[pl.ds(2 * lanes * tile + 1, lanes, stride=2), :]
     half = even.shape[1] // 2
@@ -79,15 +90,10 @@
     top = jnp.concatenate((basis, basis), axis=1)
     wide = jnp.concatenate((top, jnp.concatenate((basis, -basis), axis=1)), axis=0)
     high, low = split(dot3(jnp.concatenate((real, imag), axis=0), wide))
-    fine_c, fine_s = fcos_ref[...], fsin_ref[...]
-    for step in range(steps):
-        turn_c, turn_s = base_c[step:step + 1], base_s[step:step + 1]
-        lookup_c = turn_c * fine_c - turn_s * fine_s
-        lookup_s = -(turn_s * fine_c + turn_c * fine_s)
-        lookup_high, lookup_low = split(jnp.concatenate((lookup_c, lookup_s), axis=1))
-        temps = dot(jnp.concatenate((lookup_high, lookup_low), axis=0), high)
-        temps = temps[:points] + temps[points:] + dot(lookup_high, low)
-        at = pl.ds(step * points, points)
+    for step in range(temps_ref.shape[0] // FINE):
+        at = pl.ds(step * FINE, FINE)
+        lookup_high = high_ref[at, :]
+        temps = dot(lookup_high, high) + (dot(low_ref[at, :], high) + dot(lookup_high, low))
         if tile == 0:
             temps_ref[at, :] = temps
         else:
@@ -95,13 +101,13 @@
 
 
 def exchange_kernel(
-    n, waves, count_ref, coef_hbm, leg_ref, basis_ref, temps_ref, coef_ref, turn_ref, raw_ref, send_ref, seed_ref,
-    wide_ref, sums_ref, near_ref, side_ref, far_ref, up_ref, spectra_ref, fcos_ref, fsin_ref, coef_sem, seed_send, seed_recv,
-    near_send, near_recv, side_send, side_recv, far_send, far_recv, up_recv, diag_send,
+    n, waves, cut, count_ref, coef_hbm, leg_hbm, basis_hbm, temps_ref, coef_ref, leg_ref, basis_ref, turn_ref, raw_ref, send_ref, seed_ref,
+    wide_ref, sums_ref, near_ref, side_ref, far_ref, up_ref, spectra_ref, fcos_ref, fsin_ref, high_ref, low_ref, coef_sem, leg_sem, basis_sem, seed_send, seed_recv,
+    near_send, near_recv, side_send, side_recv, last_send, last_recv, far_send, far_recv, up_recv, lone_send, lone_recv,
 ):
     me, core, side, layer = place_in_ring(n)
     layers = n // 4
-    chunks = n
+    units = n * cut
     chip = me // 2
     rows = n
     columns = coef_hbm.shape[1]
@@ -111,12 +117,16 @@
     pairs = lanes // rows
     per = pairs // 2
     own = waves // n
-    groups = own // per
+    groups = own // (per * cut)
     depth = per * slots * 2
     part = groups * pairs
-    room = seed_ref.shape[1] // 2
+    room = seed_ref.shape[1] // (2 * cut)
+    block = seed_ref.shape[1]
     partner = me + 1 - 2 * core
     across = me + 2 - 4 * side
+    both = cut * (n - 2 * (2 * layer + 1))
+    mine = cut * (n - 4 * layer)
+    lag = 5
 
     def spot(z, y, c):
         return (z * 2 + y) * 2 + c
@@ -130,30 +140,73 @@
     def seed_copy(source, target):
         return remote(send_ref.at[target], seed_ref.at[source], seed_send.at[target], seed_recv.at[source], target)
 
-    def near_copy(q):
-        return remote(sums_ref.at[q, 1 - core], near_ref.at[q], near_send.at[q], near_recv.at[q], partner)
-
-    def side_copy(q, z):
+    def near_copy(q, t):
+        ring = near_send.shape[0]
+        return remote(sums_ref.at[q, 1 - core], near_ref.at[q], near_send.at[t % ring], near_recv.at[t % ring], partner)
+
+    def side_copy(q, z, t):
+        at = t % side_recv.shape[0]
+        return remote(sums_ref.at[q, core, 1 - side, z], side_ref.at[q, z], side_send.at[0], side_recv.at[at], across)
+
+    def side_come(q, t):
+        return remote(rest_of(side_ref.at[q]), rest_of(side_ref.at[q]), side_send.at[0], side_recv.at[t % side_recv.shape[0]], across)
+
+    def last_copy(q):
         return remote(
-            sums_ref.at[q, core, 1 - side, z], side_ref.at[q, z], side_send.at[q, z], side_recv.at[q, z], across
+            sums_ref.at[q, core, 1 - side, layer], side_ref.at[q, layer], last_send.at[0], last_recv.at[q // cut], across
         )
 
-    def far_copy(q, source, target):
+    def last_come(c):
+        both_units = side_ref.at[pl.ds(c * cut, cut), layer]
+        return remote(both_units, both_units, last_send.at[0], last_recv.at[c], across)
+
+    def lone(q):
+        return q - both
+
+    def lone_copy(q, z):
         return remote(
-            sums_ref.at[q, core, side, target], far_ref.at[source, q],
-            far_send.at[target, q], far_recv.at[source, q], spot(target, side, core),
+            sums_ref.at[q, core, 1 - side, z], side_ref.at[q, z], lone_send.at[lone(q)], lone_recv.at[lone(q)], across
         )
+
+    def lone_come(q):
+        return remote(rest_of(side_ref.at[q]), rest_of(side_ref.at[q]), lone_send.at[lone(q)], lone_recv.at[lone(q)], across)
+
+    def rest_of(ref):
+        return ref.at[pl.ds(0, layers - 1)]
+
+    def far_slot(q, target):
+        return far_recv.at[(layer - target + layers) % layers - 1, q // cut]
+
+    def far_copy(q, target):
+        return remote(
+            sums_ref.at[q, core, side, target], far_ref.at[layer, q],
+            far_send.at[0], far_slot(q, target), spot(target, side, core),
+        )
+
+    def far_come(c, source, dz):
+        both_units = far_ref.at[source, pl.ds(c * cut, cut)]
+        return remote(both_units, both_units, far_send.at[0], far_recv.at[dz - 1, c], across)
 
     def up_copy(q, target):
         return remote(
             sums_ref.at[q, core, side, target], up_ref.at[q, target],
-            far_send.at[target, q], up_recv.at[q, target], spot((layer + 1) % layers, side, core),
+            far_send.at[0], up_recv.at[q], spot((layer + 1) % layers, side, core),
         )
+
+    def up_come(q, lower):
+        pieces = up_ref.at[q, pl.ds(lower + 1, layers - 1 - lower)]
+        return remote(pieces, pieces, far_send.at[0], up_recv.at[q], across)
 
     def diag_copy(q, target):
         return remote(
             sums_ref.at[q, core, 1 - side, target], far_ref.at[layer, q],
-            diag_send.at[target, q], far_recv.at[layer, q], spot(target, 1 - side, core),
+            lone_send.at[lone(q)], far_slot(q, target), spot(target, 1 - side, core),
+        )
+
+    def relay_copy(q, target):
+        return remote(
+            side_ref.at[q, target], far_ref.at[layer, q],
+            lone_send.at[lone(q)], far_slot(q, target), spot(target, side, core),
         )
 
     def signal(target):
@@ -165,8 +218,14 @@
         dy, dc = offset
         return spot(z, (side + dy) % 2, (core + dc) % 2)
 
-    coef_copy = pltpu.make_async_copy(coef_hbm, coef_ref, coef_sem)
-    coef_copy.start()
+    pieces = coef_sem.shape[0]
+    share = n // pieces
+
+    def coef_copy(q):
+        size = share * cut * groups * depth
+        at = pl.ds(pl.multiple_of(q * size, size), size)
+        return pltpu.make_async_copy(coef_hbm.at[at, :], coef_ref.at[at, :], coef_sem.at[q])
+
     barrier = pltpu.get_barrier_semaphore()
     for offset in corners[1:]:
         signal(corner(layer, offset))
@@ -177,6 +236,17 @@
             for offset in corners:
                 signal(corner(1 + (layer - 1 + dz) % (layers - 1), offset))
 
+    leg_copy = pltpu.make_async_copy(leg_hbm, leg_ref, leg_sem)
+    leg_copy.start()
+
+    for q in range(pieces):
+        @pl.when(me + q * share < n)
+        def _():
+            coef_copy(q).start()
+
+    basis_copy = pltpu.make_async_copy(basis_hbm, basis_ref, basis_sem)
+    basis_copy.start()
+
     row = lax.broadcasted_iota(jnp.int32, (lanes, lanes), 0)
     lane = lax.broadcasted_iota(jnp.int32, (lanes, lanes), 1)
     row_at = row % rows
@@ -184,10 +254,12 @@
     moves = jnp.where(ordered * pairs + row // rows == lane, 1.0, 0.0).astype(BF16)
 
     raw_ref[...] = jnp.zeros(raw_ref.shape, F32)
-    for g in range(groups):
+    leg_copy.wait()
+    for g in range(cut * groups):
+        at = (g // groups) * 2 * room + g % groups
         turn_ref[...] = jnp.transpose(leg_ref[pl.ds(g * lanes, lanes), :])
-        raw_ref[pl.ds(g, n, stride=2 * room), :] = turn_ref[pl.ds(0, n, stride=slots), :]
-        raw_ref[pl.ds(room + g, n, stride=2 * room), :] = turn_ref[pl.ds(1, n, stride=slots), :]
+        raw_ref[pl.ds(at, n, stride=block), :] = turn_ref[pl.ds(0, n, stride=slots), :]
+        raw_ref[pl.ds(at + room, n, stride=block), :] = turn_ref[pl.ds(1, n, stride=slots), :]
     start = jnp.broadcast_to(raw_ref[pl.ds(0, 1), :], (8, lanes))
     cosine = pltpu.roll(start, lanes - rows, 1) / start
     sine = pltpu.roll(start, lanes - 2 * rows, 1) / start
@@ -199,7 +271,7 @@
         square = square + pltpu.roll(square, shift, 1)
         shift *= 2
     square = jnp.where(me == 0, square, 0.0)
-    raw_ref[pl.ds(groups, n, stride=2 * room), :] = jnp.broadcast_to(square[:1], (n, lanes))
+    raw_ref[pl.ds(groups, n, stride=block), :] = jnp.broadcast_to(square[:1], (n, lanes))
     raw = raw_ref[...]
     high = raw.astype(BF16)
     rest = raw - high.astype(F32)
@@ -243,16 +315,16 @@
                 for offset in corners:
                     give_seeds(dz, offset)
 
-    coef_copy.wait()
-
     expand_row = lax.broadcasted_iota(jnp.int32, (depth, lanes), 0)
     expand_lane = lax.broadcasted_iota(jnp.int32, (depth, lanes), 1) % pairs
     keep = (expand_row // (2 * slots)) * 2 + expand_row % 2 == expand_lane
     pair_at = lax.broadcasted_iota(jnp.int32, (room, lanes), 1) % pairs
     order_part = lax.broadcasted_iota(jnp.int32, (room, lanes), 0) * per + pair_at // 2
 
-    def recur(owner):
-        order = order_part + owner * own
+    def recur(u):
+        owner = u // cut
+        at = pl.multiple_of((u % cut) * (2 * room), 2 * room)
+        order = order_part + u * (groups * per)
         first = order + pair_at % 2 + me * (2 * slots)
         m = order.astype(F32)
         square = seed_ref[0, pl.ds(groups, 1), :]
@@ -267,8 +339,8 @@
             wide_ref[pl.ds(2 * s, room, stride=2 * slots), :] = value
             wide_ref[pl.ds(2 * s + 1, room, stride=2 * slots), :] = value
 
-        before = seed_ref[owner, pl.ds(0, room), :]
-        now = seed_ref[owner, pl.ds(room, room), :]
+        before = seed_ref[owner, pl.ds(at, room), :]
+        now = seed_ref[owner, pl.ds(at + room, room), :]
         place(0, before)
         place(1, now)
         degree = first.astype(F32)
@@ -284,75 +356,100 @@
             last = two
             place(s + 1, now)
 
-    def partial(owner):
+    def partial(u):
+        owner = u // cut
+
         @pl.when(me + owner < n)
         def _():
-            @pl.when(owner != me)
-            def _():
-                seed_copy(owner, me).wait_recv()
-
-            recur(owner)
-
-            @pl.loop(0, groups // 2)
-            def _(double):
-                for half in range(2):
-                    g = double * 2 + half
-                    at = owner * groups + g
-                    values = coef_ref[pl.ds(pl.multiple_of(at * depth, depth), depth), :]
-                    one = wide_ref[pl.ds(pl.multiple_of(g * 2 * slots, 2 * slots), 2 * slots), :]
-                    tiled = jnp.where(keep, jnp.concatenate([one] * per, axis=0), 0.0)
-                    both = jnp.concatenate(split(tiled), axis=1)
-                    sums = lax.dot_general(both, values, (((0,), (0,)), ((), ())), preferred_element_type=F32)
-                    sums = (sums[:lanes] + sums[lanes:]).reshape(2, 2, layers, pairs, columns)
-                    sums_ref[owner, :, :, :, pl.ds(pl.multiple_of(g * pairs, pairs), pairs), :] = sums
+            @pl.when(u % cut == 0)
+            def _():
+                @pl.when(owner % share == 0)
+                def _():
+                    coef_copy(owner // share).wait()
+
+                @pl.when(owner != me)
+                def _():
+                    seed_copy(owner, me).wait_recv()
+
+            recur(u)
+            for g in range(groups):
+                at = u * groups + g
+                values = coef_ref[pl.ds(pl.multiple_of(at * depth, depth), depth), :]
+                one = wide_ref[pl.ds(g * 2 * slots, 2 * slots), :]
+                tiled = jnp.where(keep, jnp.concatenate([one] * per, axis=0), 0.0)
+                both = jnp.concatenate(split(tiled), axis=1)
+                sums = lax.dot_general(both, values, (((0,), (0,)), ((), ())), preferred_element_type=F32)
+                sums = (sums[:lanes] + sums[lanes:]).reshape(2, 2, layers, pairs, columns)
+                sums_ref[u, :, :, :, pl.ds(g * pairs, pairs), :] = sums
 
         @pl.when(me + owner >= n)
         def _():
-            sums_ref[owner] = jnp.zeros((2, 2, layers, part, columns), F32)
+            sums_ref[u] = jnp.zeros((2, 2, layers, part, columns), F32)
 
     def held(q, place):
-        return q + 2 * place < chunks
-
-    def compute(q):
+        return q // cut + 2 * place < n
+
+    def compute(q, t):
         @pl.when(held(q, chip))
         def _():
             partial(q)
-            near_copy(q).start()
-
-    def merge_near(q):
-        shared = jnp.logical_and(held(q, chip), held(q, across // 2))
+
+            @pl.when(t >= near_send.shape[0])
+            def _():
+                near_copy(q, t).wait_send()
+
+            near_copy(q, t).start()
+
+    def merge_near(q, t):
+        shared = held(q, across // 2)
 
         @pl.when(held(q, chip))
         def _():
-            near_copy(q).wait_recv()
+            near_copy(q, t).wait_recv()
 
             for y in (0, 1):
                 @pl.loop(0, layers)
                 def _(z):
                     sums_ref[q, core, y, z] += near_ref[q, y, z]
 
-        @pl.when(shared)
-        def _():
-            for dz in reversed(range(1, layers)):
-                side_copy(q, (layer + dz) % layers).start()
-
-    def pass_on(q):
+            @pl.when(shared)
+            def _():
+                for dz in reversed(range(1, layers)):
+                    side_copy(q, (layer + dz) % layers, t).start()
+
+            @pl.when(jnp.logical_not(shared))
+            def _():
+                @pl.when(layer > 0)
+                def _():
+                    for dz in range(1, layers):
+                        lone_copy(q, (layer + dz) % layers).start()
+
+                last_copy(q).start()
+
+    def pass_on(q, t):
         shared = held(q, across // 2)
 
         @pl.when(held(q, chip))
         def _():
+            @pl.when(shared)
+            def _():
+                side_come(q, t).wait_recv()
+
+            for lower in range(1, layers - 1):
+                @pl.when(layer == lower)
+                def _():
+                    up_come(q, lower).wait_recv()
+
             for dz in reversed(range(1, layers)):
                 z = (layer + dz) % layers
                 upward = jnp.logical_and(z > layer + 1, held(q, chip + 2))
 
                 @pl.when(shared)
                 def _():
-                    side_copy(q, z).wait_recv()
                     sums_ref[q, core, side, z] += side_ref[q, z]
 
                 @pl.when(jnp.logical_and(layer > 0, z > layer))
                 def _():
-                    up_copy(q, z).wait_recv()
                     sums_ref[q, core, side, z] += up_ref[q, z]
 
                 @pl.when(upward)
@@ -361,77 +458,89 @@
 
                 @pl.when(jnp.logical_not(upward))
                 def _():
-                    far_copy(q, layer, z).start()
-
-                @pl.when(jnp.logical_not(shared))
-                def _():
-                    diag_copy(q, z).start()
-
-    lag = 3
-
-    @pl.loop(0, chunks + lag)
+                    far_copy(q, z).start()
+
+            @pl.when(jnp.logical_and(jnp.logical_not(shared), layer == 0))
+            def _():
+                for dz in reversed(range(1, layers)):
+                    diag_copy(q, dz).start()
+
+        @pl.when(jnp.logical_and(jnp.logical_not(held(q, chip)), jnp.logical_and(shared, layer > 0)))
+        def _():
+            lone_come(q).wait_recv()
+            for dz in range(1, layers):
+                relay_copy(q, (layer + dz) % layers).start()
+
+    def unit_at(t):
+        turn = n // 2
+        block_at, place = t // turn, t % turn
+        early = jnp.where(place == turn - 1, both + block_at, block_at * (turn - 1) + place)
+        return jnp.where(layer == 0, early, t)
+
+    @pl.loop(0, units + lag)
     def _(t):
-        @pl.when(t < chunks)
-        def _():
-            compute(t)
-
-        @pl.when(t == 1)
+        @pl.when(t == lag)
         def _():
             meet()
 
-        @pl.when(jnp.logical_and(t >= 1, t <= chunks))
-        def _():
-            merge_near(t - 1)
-
-        @pl.when(t == chunks - 2 * chip)
-        def _():
-            @pl.loop(0, chunks)
+        @pl.when(t < units)
+        def _():
+            compute(unit_at(t), t)
+
+        @pl.when(jnp.logical_and(t >= 1, t <= units))
+        def _():
+            merge_near(unit_at(t - 1), t - 1)
+
+        @pl.when(t == mine)
+        def _():
+            @pl.loop(0, both)
             def _(q):
-                @pl.when(held(q, chip))
-                def _():
-                    side_copy(q, layer).start()
+                last_copy(q).start()
 
         @pl.when(t >= lag)
         def _():
-            pass_on(t - lag)
-
-    def finish(q):
-        at = pl.ds(pl.multiple_of(q * part, part), part)
-
-        @pl.when(held(q, chip))
-        def _():
-            spectra_ref[at, :] = sums_ref[q, core, side, layer]
-
-        @pl.when(jnp.logical_not(held(q, chip)))
-        def _():
-            spectra_ref[at, :] = jnp.zeros((part, columns), F32)
+            pass_on(unit_at(t - lag), t - lag)
+
+    def finish(c):
+        near_part = held(c * cut, chip)
 
         for dz in range(1, layers):
             source = (layer + dz) % layers
-
-            passed = jnp.logical_and(source + 1 < layer, held(q, 2 * (source + 1) + side))
-
-            @pl.when(jnp.logical_and(held(q, 2 * source), jnp.logical_not(passed)))
-            def _():
-                far_copy(q, source, layer).wait_recv()
-                spectra_ref[at, :] += far_ref[source, q]
-
-        @pl.when(held(q, across // 2))
-        def _():
-            side_copy(q, layer).wait_recv()
-            spectra_ref[at, :] += side_ref[q, layer]
-
-    tiles = waves // lanes
-    done = 0
-    for tile in range(tiles):
-        until = -(-(tile + 1) * lanes // own)
-
-        @pl.loop(done, until)
-        def _(q):
-            finish(q)
-
-        done = until
-        trig_tile(tile, count_ref[0], spectra_ref, basis_ref, fcos_ref, fsin_ref, temps_ref)
+            passed = jnp.logical_and(source + 1 < layer, held(c * cut, 2 * (source + 1) + side))
+
+            @pl.when(jnp.logical_and(held(c * cut, 2 * source), jnp.logical_not(passed)))
+            def _():
+                far_come(c, source, dz).wait_recv()
+
+        @pl.when(held(c * cut, across // 2))
+        def _():
+            last_come(c).wait_recv()
+
+        for half in range(cut):
+            q = c * cut + half
+            at = pl.ds(pl.multiple_of(q * part, part), part)
+
+            @pl.when(near_part)
+            def _():
+                spectra_ref[at, :] = sums_ref[q, core, side, layer]
+
+            @pl.when(jnp.logical_not(near_part))
+            def _():
+                spectra_ref[at, :] = jnp.zeros((part, columns), F32)
+
+            for dz in range(1, layers):
+                source = (layer + dz) % layers
+                passed = jnp.logical_and(source + 1 < layer, held(q, 2 * (source + 1) + side))
+
+                @pl.when(jnp.logical_and(held(q, 2 * source), jnp.logical_not(passed)))
+                def _():
+                    spectra_ref[at, :] += far_ref[source, q]
+
+            @pl.when(held(q, across // 2))
+            def _():
+                spectra_ref[at, :] += side_ref[q, layer]
+
+    ring = near_send.shape[0]
 
     @pl.loop(0, n)
     def _(target):
@@ -439,23 +548,45 @@
         def _():
             seed_copy(me, target).wait_send()
 
-    @pl.loop(0, chunks)
-    def _(q):
-        @pl.when(held(q, chip))
-        def _():
-            near_copy(q).wait_send()
-            side_copy(q, layer).wait_send()
-            for dz in range(1, layers):
-                z = (layer + dz) % layers
-                far_copy(q, layer, z).wait_send()
-
-                @pl.when(held(q, across // 2))
-                def _():
-                    side_copy(q, z).wait_send()
-
-                @pl.when(jnp.logical_not(held(q, across // 2)))
-                def _():
-                    diag_copy(q, z).wait_send()
+    @pl.loop(0, ring)
+    def _(k):
+        @pl.when(held(unit_at(k), chip))
+        def _():
+            near_copy(k, k).wait_send()
+
+    tiles = waves // lanes
+    done = 0
+    basis_copy.wait()
+    for tile in range(tiles):
+        until = -(-(tile + 1) * lanes // own)
+        fill_lookup(tile, count_ref[0], fcos_ref, fsin_ref, high_ref, low_ref)
+
+        @pl.loop(done, until)
+        def _(c):
+            finish(c)
+
+        done = until
+        add_tile(tile, spectra_ref, basis_ref, high_ref, low_ref, temps_ref)
+
+    for place in range(n // 2):
+        count = cut * (n - 2 * place)
+        pair = cut * (n - 2 * (place // 2 * 2 + 1))
+
+        @pl.when(chip == place)
+        def _():
+            side = side_ref.at[pl.ds(0, pair), pl.ds(0, layers - 1)]
+            remote(side, side, side_send.at[0], side_recv.at[0], across).wait_send()
+            last = side_ref.at[pl.ds(0, count), 0]
+            remote(last, last, last_send.at[0], last_recv.at[0], across).wait_send()
+            far = far_ref.at[pl.ds(0, layers - 1), pl.ds(0, count)]
+            remote(far, far, far_send.at[0], far_recv.at[0, 0], across).wait_send()
+
+    sends_lone = jnp.logical_or(side == 0, layer > 0)
+
+    @pl.when(sends_lone)
+    def _():
+        for k in range(lone_send.shape[0]):
+            remote(rest_of(side_ref.at[0]), rest_of(side_ref.at[0]), lone_send.at[k], lone_recv.at[k], across).wait_send()
 
 
 def exchanged_temps(coefficients, legendre, row_counts, basis, n, points):
@@ -463,41 +594,49 @@
     own, _, every, rows = legendre.shape
     dense = jnp.transpose(coefficients, (0, 2, 1, 3)).reshape(waves * slots * 2, columns)
     legs = jnp.transpose(legendre, (0, 1, 3, 2)).reshape(own * 2 * rows, every)
-    layers, chunks = n // 4, n
+    layers = n // 4
     pairs = LANES // rows
     groups = own * 2 // pairs
-    width = groups * pairs
-    room = -(-(groups + 1) // 8) * 8
+    cut = 2 if groups % 2 == 0 else 1
+    units = n * cut
+    width = groups // cut * pairs
+    room = -(-(groups // cut + 1) // 8) * 8
+    block = cut * 2 * room
     dma = pltpu.SemaphoreType.DMA
 
     def body(*refs):
-        exchange_kernel(n, waves, *refs)
+        exchange_kernel(n, waves, cut, *refs)
 
     vmem = pl.BlockSpec(memory_space=pltpu.VMEM)
     return pl.pallas_call(
         body,
         out_shape=jax.ShapeDtypeStruct((points, 2 * basis.shape[1]), F32),
-        in_specs=[pl.BlockSpec(memory_space=pltpu.SMEM), pl.BlockSpec(memory_space=pl.ANY), vmem, vmem],
+        in_specs=[pl.BlockSpec(memory_space=pltpu.SMEM)] + [pl.BlockSpec(memory_space=pl.ANY)] * 3,
         out_specs=vmem,
         scratch_shapes=[
             pltpu.VMEM(dense.shape, BF16),
+            pltpu.VMEM(legs.shape, F32),
+            pltpu.VMEM(basis.shape, F32),
             pltpu.VMEM((every, LANES), F32),
-            pltpu.VMEM((n * 2 * room, LANES), F32),
-            pltpu.VMEM((n, 2 * room, LANES), F32),
-            pltpu.VMEM((n, 2 * room, LANES), F32),
+            pltpu.VMEM((n * block, LANES), F32),
+            pltpu.VMEM((n, block, LANES), F32),
+            pltpu.VMEM((n, block, LANES), F32),
             pltpu.VMEM((room * 2 * slots, LANES), F32),
-            pltpu.VMEM((chunks, 2, 2, layers, width, columns), F32),
-            pltpu.VMEM((chunks, 2, layers, width, columns), F32),
-            pltpu.VMEM((chunks, layers, width, columns), F32),
-            pltpu.VMEM((layers, chunks, width, columns), F32),
-            pltpu.VMEM((chunks, layers, width, columns), F32),
+            pltpu.VMEM((units, 2, 2, layers, width, columns), F32),
+            pltpu.VMEM((units, 2, layers, width, columns), F32),
+            pltpu.VMEM((units, layers, width, columns), F32),
+            pltpu.VMEM((layers, units, width, columns), F32),
+            pltpu.VMEM((units, layers, width, columns), F32),
             pltpu.VMEM((2 * waves, columns), F32),
             pltpu.VMEM((FINE, LANES), F32),
             pltpu.VMEM((FINE, LANES), F32),
-            dma, dma((n,)), dma((n,)),
-            dma((chunks,)), dma((chunks,)),
-            dma((chunks, layers)), dma((chunks, layers)),
-            dma((layers, chunks)), dma((layers, chunks)), dma((chunks, layers)), dma((layers, chunks)),
+            pltpu.VMEM((points, 2 * LANES), BF16),
+            pltpu.VMEM((points, 2 * LANES), BF16),
+            dma((n // 2,)), dma, dma, dma((n,)), dma((n,)),
+            dma((8,)), dma((8,)),
+            dma((1,)), dma((16,)),
+            dma((1,)), dma((n,)),
+            dma((1,)), dma((layers - 1, n)), dma((units - 4 * cut,)), dma((2 * cut,)), dma((2 * cut,)),
         ],
         compiler_params=pltpu.CompilerParams(
             collective_id=0, has_side_effects=True, vmem_limit_bytes=58 * 1024 * 1024
@@ -509,9 +648,10 @@
 def plain_temps(spectra, row_counts, basis, points):
     tiles = spectra.shape[0] // (2 * LANES)
 
-    def body(count_ref, spectra_ref, basis_ref, temps_ref, fcos_ref, fsin_ref):
+    def body(count_ref, spectra_ref, basis_ref, temps_ref, fcos_ref, fsin_ref, high_ref, low_ref):
         for tile in range(tiles):
-            trig_tile(tile, count_ref[0], spectra_ref, basis_ref, fcos_ref, fsin_ref, temps_ref)
+            fill_lookup(tile, count_ref[0], fcos_ref, fsin_ref, high_ref, low_ref)
+            add_tile(tile, spectra_ref, basis_ref, high_ref, low_ref, temps_ref)
 
     vmem = pl.BlockSpec(memory_space=pltpu.VMEM)
     return pl.pallas_call(
@@ -519,7 +659,7 @@
         out_shape=jax.ShapeDtypeStruct((points, 2 * basis.shape[1]), F32),
         in_specs=[pl.BlockSpec(memory_space=pltpu.SMEM), vmem, vmem],
         out_specs=vmem,
-        scratch_shapes=[pltpu.VMEM((FINE, LANES), F32), pltpu.VMEM((FINE, LANES), F32)],
+        scratch_shapes=[pltpu.VMEM((FINE, LANES), F32)] * 2 + [pltpu.VMEM((points, 2 * LANES), BF16)] * 2,
         name="plain_temps",
     )(row_counts, spectra, basis)
 

time: 81.4 us -> 73.8 us (0.907)
  the two profiles are of different devices: /device:TPU:5 before, /device:TPU:12 now
where the time goes in v3:
time: 73.8 us; the launch traced here: 73.4 us
  Pallas kernels  72.8 us (99%)
    pallas_call x1, Pallas kernels, exchanged_temps(): pl.pallas_call(body, out_shape=jax.ShapeDtypeStruct((points, 2 * basis.sh...  66.2 us
    pallas_call x1, Pallas kernels, radiate_row(): pl.pallas_call(row_kernel, out_shape=jax.ShapeDtypeStruct((1, 2, points,...  6.54 us

profile of v3, /device:TPU:12, one launch (start us, length us, event | category | flops | bytes accessed | tf_op | source)
XLA Modules:
  0.0 73.4 jit_solution(374134510868904676)
XLA Ops:
  0.7 66.2 %exchanged_temps.1.temps_ref = f32[1280,256]{1,0:T(8,128)} custom-call(s32[1]{0:T(128)S(6)} %copy.8.refs_0_.count_ref, bf16[25600,128]{1,0:T(8,128)(2,1)} %bitcast.9, f32[1280,320]{1,0:T(8,128)} %bitcast.10, f32[64,128]{1,0:T(8,128)} %refs_3_.1), custom_call_target="tpu_custom_call" | custom-call | tf_op jit(solution)/shard_map/exchanged_temps/pallas_call | solution.py:611
  66.9 6.5 %row_radiance.1 = f32[1,2,1280,512]{3,2,1,0:T(8,128)} custom-call(s32[1]{0:T(128)S(6)} %copy.8.refs_0_.count_ref, f32[1280,256]{1,0:T(8,128)} %exchanged_temps.1.temps_ref, f32[1,128]{1,0:T(1,128)} %bitcast.13, s32[1,512]{1,0:T(1,128)} %bitcast.11, f32[1,512]{1,0:T(1,128)} %bitcast.12), custom_call_target="tpu_custom_call" | custom-call | tf_op jit(solution)/shard_map/row_radiance/pallas_call | solution.py:709

commit v4 on v3

--- a/solution.py
+++ b/solution.py
@@ -9,6 +9,7 @@
 
 NLON = 1280
 FINE = 256
+SPAN = 640
 LANES = 128
 
 PRECISE = lax.Precision.HIGHEST
@@ -48,7 +49,7 @@
 
 def fill_lookup(tile, count, fcos_ref, fsin_ref, high_ref, low_ref):
     points, lanes = fcos_ref.shape
-    steps = high_ref.shape[0] // points
+    steps = high_ref.shape[1] // points
     tiny = 16
     middle = points // tiny
     coarse = -(-steps // 8) * 8
@@ -75,14 +76,15 @@
         lookup_c = turn_c * fine_c - turn_s * fine_s
         lookup_s = -(turn_s * fine_c + turn_c * fine_s)
         high, low = split(jnp.concatenate((lookup_c, lookup_s), axis=1))
-        high_ref[pl.ds(step * points, points), :] = high
-        low_ref[pl.ds(step * points, points), :] = low
-
-
-def add_tile(tile, spectra_ref, basis_ref, high_ref, low_ref, temps_ref):
+        high_ref[tile, pl.ds(step * points, points), :] = high
+        low_ref[tile, pl.ds(step * points, points), :] = low
+
+
+def add_tile(tile, spectra_ref, basis_ref, high_ref, low_ref, temps_ref, after=None):
     lanes = LANES
-    even = spectra_ref[pl.ds(2 * lanes * tile, lanes, stride=2), :]
-    odd = spectra_ref[pl.ds(2 * lanes * tile + 1, lanes, stride=2), :]
+    first = 2 * lanes * tile
+    even = spectra_ref[pl.ds(first, lanes, stride=2), :]
+    odd = spectra_ref[pl.ds(first + 1, lanes, stride=2), :]
     half = even.shape[1] // 2
     real = jnp.concatenate((even[:, :half], odd[:, :half]), axis=1)
     imag = jnp.concatenate((even[:, half:], odd[:, half:]), axis=1)
@@ -92,17 +94,15 @@
     high, low = split(dot3(jnp.concatenate((real, imag), axis=0), wide))
     for step in range(temps_ref.shape[0] // FINE):
         at = pl.ds(step * FINE, FINE)
-        lookup_high = high_ref[at, :]
-        temps = dot(lookup_high, high) + (dot(low_ref[at, :], high) + dot(lookup_high, low))
-        if tile == 0:
-            temps_ref[at, :] = temps
-        else:
-            temps_ref[at, :] += temps
+        lookup_high = high_ref[tile, at, :]
+        temps_ref[at, :] += dot(lookup_high, high) + (dot(low_ref[tile, at, :], high) + dot(lookup_high, low))
+        if after is not None:
+            after(step)
 
 
 def exchange_kernel(
-    n, waves, cut, count_ref, coef_hbm, leg_hbm, basis_hbm, temps_ref, coef_ref, leg_ref, basis_ref, turn_ref, raw_ref, send_ref, seed_ref,
-    wide_ref, sums_ref, near_ref, side_ref, far_ref, up_ref, spectra_ref, fcos_ref, fsin_ref, high_ref, low_ref, coef_sem, leg_sem, basis_sem, seed_send, seed_recv,
+    n, waves, cut, count_ref, coef_hbm, leg_hbm, basis_hbm, out_hbm, temps_ref, coef_ref, leg_ref, basis_ref, turn_ref, raw_ref, send_ref, seed_ref,
+    wide_ref, sums_ref, near_ref, side_ref, far_ref, up_ref, spectra_ref, fcos_ref, fsin_ref, high_ref, low_ref, coef_sem, leg_sem, basis_sem, out_sem, seed_send, seed_recv,
     near_send, near_recv, side_send, side_recv, last_send, last_recv, far_send, far_recv, up_recv, lone_send, lone_recv,
 ):
     me, core, side, layer = place_in_ring(n)
@@ -239,11 +239,6 @@
     leg_copy = pltpu.make_async_copy(leg_hbm, leg_ref, leg_sem)
     leg_copy.start()
 
-    for q in range(pieces):
-        @pl.when(me + q * share < n)
-        def _():
-            coef_copy(q).start()
-
     basis_copy = pltpu.make_async_copy(basis_hbm, basis_ref, basis_sem)
     basis_copy.start()
 
@@ -255,6 +250,11 @@
 
     raw_ref[...] = jnp.zeros(raw_ref.shape, F32)
     leg_copy.wait()
+    for q in range(pieces):
+        @pl.when(me + q * share < n)
+        def _():
+            coef_copy(q).start()
+
     for g in range(cut * groups):
         at = (g // groups) * 2 * room + g % groups
         turn_ref[...] = jnp.transpose(leg_ref[pl.ds(g * lanes, lanes), :])
@@ -307,6 +307,17 @@
             for offset in corners:
                 give_seeds((layer + dz) % layers, offset)
 
+    tiles = waves // lanes
+
+    def fill(tile):
+        fill_lookup(tile, count_ref[0], fcos_ref, fsin_ref, high_ref, low_ref)
+
+    @pl.when(layer > 0)
+    def _():
+        @pl.loop(0, tiles)
+        def _(tile):
+            fill(tile)
+
     def meet():
         @pl.when(layer == 0)
         def _():
@@ -477,12 +488,71 @@
         early = jnp.where(place == turn - 1, both + block_at, block_at * (turn - 1) + place)
         return jnp.where(layer == 0, early, t)
 
+    def finish(c):
+        near_part = held(c * cut, chip)
+
+        for dz in range(1, layers):
+            source = (layer + dz) % layers
+            passed = jnp.logical_and(source + 1 < layer, held(c * cut, 2 * (source + 1) + side))
+
+            @pl.when(jnp.logical_and(held(c * cut, 2 * source), jnp.logical_not(passed)))
+            def _():
+                far_come(c, source, dz).wait_recv()
+
+        @pl.when(held(c * cut, across // 2))
+        def _():
+            last_come(c).wait_recv()
+
+        for half in range(cut):
+            q = c * cut + half
+            at = pl.ds(pl.multiple_of(q * part, part), part)
+
+            @pl.when(near_part)
+            def _():
+                spectra_ref[at, :] = sums_ref[q, core, side, layer]
+
+            @pl.when(jnp.logical_not(near_part))
+            def _():
+                spectra_ref[at, :] = jnp.zeros((part, columns), F32)
+
+            for dz in range(1, layers):
+                source = (layer + dz) % layers
+                passed = jnp.logical_and(source + 1 < layer, held(q, 2 * (source + 1) + side))
+
+                @pl.when(jnp.logical_and(held(q, 2 * source), jnp.logical_not(passed)))
+                def _():
+                    spectra_ref[at, :] += far_ref[source, q]
+
+            @pl.when(held(q, across // 2))
+            def _():
+                spectra_ref[at, :] += side_ref[q, layer]
+
+    temps_ref[...] = jnp.zeros(temps_ref.shape, F32)
+    basis_copy.wait()
+
+    def out_copy(step):
+        at = pl.ds(step * FINE, FINE)
+        return pltpu.make_async_copy(temps_ref.at[at, :], out_hbm.at[at, :], out_sem.at[step])
+
+    def stage(tile, after=None):
+        @pl.loop((tile * lanes + own - 1) // own, ((tile + 1) * lanes + own - 1) // own)
+        def _(c):
+            finish(c)
+
+        add_tile(tile, spectra_ref, basis_ref, high_ref, low_ref, temps_ref, after)
+
     @pl.loop(0, units + lag)
     def _(t):
         @pl.when(t == lag)
         def _():
             meet()
 
+        @pl.when(jnp.logical_and(layer == 0, jnp.logical_and(t >= 2 * lag, t < 2 * (lag + tiles))))
+        def _():
+            @pl.when(t % 2 == 0)
+            def _():
+                fill(t // 2 - lag)
+
         @pl.when(t < units)
         def _():
             compute(unit_at(t), t)
@@ -501,45 +571,6 @@
         def _():
             pass_on(unit_at(t - lag), t - lag)
 
-    def finish(c):
-        near_part = held(c * cut, chip)
-
-        for dz in range(1, layers):
-            source = (layer + dz) % layers
-            passed = jnp.logical_and(source + 1 < layer, held(c * cut, 2 * (source + 1) + side))
-
-            @pl.when(jnp.logical_and(held(c * cut, 2 * source), jnp.logical_not(passed)))
-            def _():
-                far_come(c, source, dz).wait_recv()
-
-        @pl.when(held(c * cut, across // 2))
-        def _():
-            last_come(c).wait_recv()
-
-        for half in range(cut):
-            q = c * cut + half
-            at = pl.ds(pl.multiple_of(q * part, part), part)
-
-            @pl.when(near_part)
-            def _():
-                spectra_ref[at, :] = sums_ref[q, core, side, layer]
-
-            @pl.when(jnp.logical_not(near_part))
-            def _():
-                spectra_ref[at, :] = jnp.zeros((part, columns), F32)
-
-            for dz in range(1, layers):
-                source = (layer + dz) % layers
-                passed = jnp.logical_and(source + 1 < layer, held(q, 2 * (source + 1) + side))
-
-                @pl.when(jnp.logical_and(held(q, 2 * source), jnp.logical_not(passed)))
-                def _():
-                    spectra_ref[at, :] += far_ref[source, q]
-
-            @pl.when(held(q, across // 2))
-            def _():
-                spectra_ref[at, :] += side_ref[q, layer]
-
     ring = near_send.shape[0]
 
     @pl.loop(0, n)
@@ -554,19 +585,11 @@
         def _():
             near_copy(k, k).wait_send()
 
-    tiles = waves // lanes
-    done = 0
-    basis_copy.wait()
-    for tile in range(tiles):
-        until = -(-(tile + 1) * lanes // own)
-        fill_lookup(tile, count_ref[0], fcos_ref, fsin_ref, high_ref, low_ref)
-
-        @pl.loop(done, until)
-        def _(c):
-            finish(c)
-
-        done = until
-        add_tile(tile, spectra_ref, basis_ref, high_ref, low_ref, temps_ref)
+    @pl.loop(0, tiles - 1)
+    def _(tile):
+        stage(tile)
+
+    stage(tiles - 1, lambda step: out_copy(step).start())
 
     for place in range(n // 2):
         count = cut * (n - 2 * place)
@@ -587,6 +610,9 @@
     def _():
         for k in range(lone_send.shape[0]):
             remote(rest_of(side_ref.at[0]), rest_of(side_ref.at[0]), lone_send.at[k], lone_recv.at[k], across).wait_send()
+
+    for step in range(out_sem.shape[0]):
+        out_copy(step).wait()
 
 
 def exchanged_temps(coefficients, legendre, row_counts, basis, n, points):
@@ -607,13 +633,13 @@
     def body(*refs):
         exchange_kernel(n, waves, cut, *refs)
 
-    vmem = pl.BlockSpec(memory_space=pltpu.VMEM)
     return pl.pallas_call(
         body,
         out_shape=jax.ShapeDtypeStruct((points, 2 * basis.shape[1]), F32),
         in_specs=[pl.BlockSpec(memory_space=pltpu.SMEM)] + [pl.BlockSpec(memory_space=pl.ANY)] * 3,
-        out_specs=vmem,
+        out_specs=pl.BlockSpec(memory_space=pl.ANY),
         scratch_shapes=[
+            pltpu.VMEM((points, 2 * basis.shape[1]), F32),
             pltpu.VMEM(dense.shape, BF16),
             pltpu.VMEM(legs.shape, F32),
             pltpu.VMEM(basis.shape, F32),
@@ -630,9 +656,9 @@
             pltpu.VMEM((2 * waves, columns), F32),
             pltpu.VMEM((FINE, LANES), F32),
             pltpu.VMEM((FINE, LANES), F32),
-            pltpu.VMEM((points, 2 * LANES), BF16),
-            pltpu.VMEM((points, 2 * LANES), BF16),
-            dma((n // 2,)), dma, dma, dma((n,)), dma((n,)),
+            pltpu.VMEM((waves // LANES, points, 2 * LANES), BF16),
+            pltpu.VMEM((waves // LANES, points, 2 * LANES), BF16),
+            dma((n // 2,)), dma, dma, dma((points // FINE,)), dma((n,)), dma((n,)),
             dma((8,)), dma((8,)),
             dma((1,)), dma((16,)),
             dma((1,)), dma((n,)),
@@ -649,6 +675,7 @@
     tiles = spectra.shape[0] // (2 * LANES)
 
     def body(count_ref, spectra_ref, basis_ref, temps_ref, fcos_ref, fsin_ref, high_ref, low_ref):
+        temps_ref[...] = jnp.zeros(temps_ref.shape, F32)
         for tile in range(tiles):
             fill_lookup(tile, count_ref[0], fcos_ref, fsin_ref, high_ref, low_ref)
             add_tile(tile, spectra_ref, basis_ref, high_ref, low_ref, temps_ref)
@@ -659,7 +686,7 @@
         out_shape=jax.ShapeDtypeStruct((points, 2 * basis.shape[1]), F32),
         in_specs=[pl.BlockSpec(memory_space=pltpu.SMEM), vmem, vmem],
         out_specs=vmem,
-        scratch_shapes=[pltpu.VMEM((FINE, LANES), F32)] * 2 + [pltpu.VMEM((points, 2 * LANES), BF16)] * 2,
+        scratch_shapes=[pltpu.VMEM((FINE, LANES), F32)] * 2 + [pltpu.VMEM((tiles, points, 2 * LANES), BF16)] * 2,
         name="plain_temps",
     )(row_counts, spectra, basis)
 
@@ -701,6 +728,7 @@
 
 def radiate_row(temps, row_counts, absorb, peak_level, width):
     points = temps.shape[0]
+    span = SPAN if points % SPAN == 0 else FINE
     levels, channels = absorb.shape[0], width.shape[0]
 
     def whole(*shape):
@@ -711,14 +739,14 @@
         out_shape=jax.ShapeDtypeStruct((1, 2, points, channels), F32),
         grid_spec=pltpu.PrefetchScalarGridSpec(
             num_scalar_prefetch=1,
-            grid=(points // FINE,),
+            grid=(points // span,),
             in_specs=[
-                pl.BlockSpec((FINE, 2 * levels), lambda i, *_: (i, 0)),
+                pl.BlockSpec((span, 2 * levels), lambda i, *_: (i, 0)),
                 whole(1, levels),
                 whole(1, channels),
                 whole(1, channels),
             ],
-            out_specs=pl.BlockSpec((1, 2, FINE, channels), lambda i, *_: (0, 0, i, 0)),
+            out_specs=pl.BlockSpec((1, 2, span, channels), lambda i, *_: (0, 0, i, 0)),
             scratch_shapes=[
                 pltpu.VMEM((2 * levels, channels), BF16),
                 pltpu.VMEM((levels, channels), BF16),

time: 73.8 us -> 71.2 us (0.965)
  Pallas kernels: 72.8 us -> 69.9 us
    pallas_call x1, Pallas kernels: 66.2 us -> 64.2 us  [exchanged_temps(): pl.pallas_call(body, out_shape=jax.ShapeDtypeStruct((points, 2 * basis.sh...]
    pallas_call x1, Pallas kernels: 6.54 us -> 5.71 us  [radiate_row(): pl.pallas_call(row_kernel, out_shape=jax.ShapeDtypeStruct((1, 2, points,...]
where the time goes in v4:
time: 71.2 us; the launch traced here: 70.6 us
  Pallas kernels  69.9 us (98%)
    pallas_call x1, Pallas kernels, exchanged_temps(): pl.pallas_call(body, out_shape=jax.ShapeDtypeStruct((points, 2 * basis.sh...  64.2 us
    pallas_call x1, Pallas kernels, radiate_row(): pl.pallas_call(row_kernel, out_shape=jax.ShapeDtypeStruct((1, 2, points,...  5.71 us

profile of v4, /device:TPU:12, one launch (start us, length us, event | category | flops | bytes accessed | tf_op | source)
XLA Modules:
  0.0 70.6 jit_solution(17490759159527430669)
XLA Ops:
  0.7 64.2 %exchanged_temps.1.temps_ref = f32[1280,256]{1,0:T(8,128)} custom-call(s32[1]{0:T(128)S(6)} %copy.8.refs_0_.count_ref, bf16[25600,128]{1,0:T(8,128)(2,1)} %bitcast.9, f32[1280,320]{1,0:T(8,128)} %bitcast.10, f32[64,128]{1,0:T(8,128)} %refs_3_.1), custom_call_target="tpu_custom_call" | custom-call | tf_op jit(solution)/shard_map/exchanged_temps/pallas_call | solution.py:636
  64.8 5.7 %row_radiance.1 = f32[1,2,1280,512]{3,2,1,0:T(8,128)} custom-call(s32[1]{0:T(128)S(6)} %copy.8.refs_0_.count_ref, f32[1280,256]{1,0:T(8,128)} %exchanged_temps.1.temps_ref, f32[1,128]{1,0:T(1,128)} %bitcast.13, s32[1,512]{1,0:T(1,128)} %bitcast.11, f32[1,512]{1,0:T(1,128)} %bitcast.12), custom_call_target="tpu_custom_call" | custom-call | tf_op jit(solution)/shard_map/row_radiance/pallas_call | solution.py:737

commit v5 on v4

--- a/solution.py
+++ b/solution.py
@@ -101,9 +101,9 @@
 
 
 def exchange_kernel(
-    n, waves, cut, count_ref, coef_hbm, leg_hbm, basis_hbm, out_hbm, temps_ref, coef_ref, leg_ref, basis_ref, turn_ref, raw_ref, send_ref, seed_ref,
-    wide_ref, sums_ref, near_ref, side_ref, far_ref, up_ref, spectra_ref, fcos_ref, fsin_ref, high_ref, low_ref, coef_sem, leg_sem, basis_sem, out_sem, seed_send, seed_recv,
-    near_send, near_recv, side_send, side_recv, last_send, last_recv, far_send, far_recv, up_recv, lone_send, lone_recv,
+    n, waves, cut, count_ref, coef_hbm, leg_hbm, basis_hbm, out_hbm, temps_ref, coef_ref, leg_ref, basis_ref, turn_ref, raw_ref, send_ref, seed_ref, hold_ref,
+    wide_ref, sums_ref, near_ref, side_ref, far_ref, up_ref, spectra_ref, fcos_ref, fsin_ref, high_ref, low_ref, coef_sem, leg_sem, basis_sem, out_sem, seed_send, seed_recv, hold_send, hold_recv,
+    near_send, near_recv, side_send, side_recv, last_send, come_recv, far_send, up_recv, lone_send, lone_recv,
 ):
     me, core, side, layer = place_in_ring(n)
     layers = n // 4
@@ -140,9 +140,20 @@
     def seed_copy(source, target):
         return remote(send_ref.at[target], seed_ref.at[source], seed_send.at[target], seed_recv.at[source], target)
 
+    def hold_copy(place, target):
+        at = spot(layer, 1 - side, place)
+        return remote(send_ref.at[target], hold_ref.at[core], seed_send.at[target], hold_recv.at[core], at)
+
+    def hold_come(k):
+        return remote(hold_ref.at[k], hold_ref.at[k], hold_send.at[k], hold_recv.at[k], across)
+
+    def hold_pass(k):
+        owner = spot(layer, 1 - side, k)
+        return remote(hold_ref.at[k], seed_ref.at[owner], hold_send.at[k], seed_recv.at[owner], spot(0, side, core))
+
     def near_copy(q, t):
-        ring = near_send.shape[0]
-        return remote(sums_ref.at[q, 1 - core], near_ref.at[q], near_send.at[t % ring], near_recv.at[t % ring], partner)
+        ring = near_recv.shape[0]
+        return remote(sums_ref.at[q, 1 - core], near_ref.at[q], near_send, near_recv.at[t % ring], partner)
 
     def side_copy(q, z, t):
         at = t % side_recv.shape[0]
@@ -153,12 +164,8 @@
 
     def last_copy(q):
         return remote(
-            sums_ref.at[q, core, 1 - side, layer], side_ref.at[q, layer], last_send.at[0], last_recv.at[q // cut], across
+            sums_ref.at[q, core, 1 - side, layer], side_ref.at[q, layer], last_send.at[0], come_recv.at[q // cut], across
         )
-
-    def last_come(c):
-        both_units = side_ref.at[pl.ds(c * cut, cut), layer]
-        return remote(both_units, both_units, last_send.at[0], last_recv.at[c], across)
 
     def lone(q):
         return q - both
@@ -168,24 +175,28 @@
             sums_ref.at[q, core, 1 - side, z], side_ref.at[q, z], lone_send.at[lone(q)], lone_recv.at[lone(q)], across
         )
 
-    def lone_come(q):
-        return remote(rest_of(side_ref.at[q]), rest_of(side_ref.at[q]), lone_send.at[lone(q)], lone_recv.at[lone(q)], across)
+    def lone_part(q, pieces):
+        part_ref = side_ref.at[q, pl.ds(0, pieces)]
+        return remote(part_ref, part_ref, lone_send.at[lone(q)], lone_recv.at[lone(q)], across)
+
+    def relayed(z, at):
+        return z != at and at > 0
+
+    def relays(at):
+        return [z for z in range(layers) if relayed(z, at)]
 
     def rest_of(ref):
         return ref.at[pl.ds(0, layers - 1)]
-
-    def far_slot(q, target):
-        return far_recv.at[(layer - target + layers) % layers - 1, q // cut]
 
     def far_copy(q, target):
         return remote(
             sums_ref.at[q, core, side, target], far_ref.at[layer, q],
-            far_send.at[0], far_slot(q, target), spot(target, side, core),
+            far_send.at[0], come_recv.at[q // cut], spot(target, side, core),
         )
 
-    def far_come(c, source, dz):
-        both_units = far_ref.at[source, pl.ds(c * cut, cut)]
-        return remote(both_units, both_units, far_send.at[0], far_recv.at[dz - 1, c], across)
+    def come(c, pieces):
+        arrived = far_ref.at[pl.ds(0, pieces), pl.ds(c * cut, cut)]
+        return remote(arrived, arrived, far_send.at[0], come_recv.at[c], across)
 
     def up_copy(q, target):
         return remote(
@@ -200,13 +211,13 @@
     def diag_copy(q, target):
         return remote(
             sums_ref.at[q, core, 1 - side, target], far_ref.at[layer, q],
-            lone_send.at[lone(q)], far_slot(q, target), spot(target, 1 - side, core),
+            lone_send.at[lone(q)], come_recv.at[q // cut], spot(target, 1 - side, core),
         )
 
     def relay_copy(q, target):
         return remote(
             side_ref.at[q, target], far_ref.at[layer, q],
-            lone_send.at[lone(q)], far_slot(q, target), spot(target, side, core),
+            lone_send.at[lone(q)], come_recv.at[q // cut], spot(target, side, core),
         )
 
     def signal(target):
@@ -301,11 +312,26 @@
         pl.semaphore_wait(barrier, n - 1)
         for offset in corners:
             signal(corner(0, offset))
+        for dy, dc in corners:
+            target = spot(0, (side + dy) % 2, (core + dc) % 2)
+
+            @pl.when(me + target < n)
+            def _():
+                if dy:
+                    hold_copy((core + dc) % 2, target).start()
+                else:
+                    seed_copy(me, target).start()
+
         for offset in corners[1:]:
             give_seeds(layer, offset)
-        for dz in range(1, layers):
+        for dz in range(1, layers - 1):
             for offset in corners:
-                give_seeds((layer + dz) % layers, offset)
+                give_seeds(1 + (layer - 1 + dz) % (layers - 1), offset)
+        for k in range(2):
+            @pl.when(spot(layer, 1 - side, k) + spot(0, side, core) < n)
+            def _():
+                hold_come(k).wait_recv()
+                hold_pass(k).start()
 
     tiles = waves // lanes
 
@@ -405,10 +431,6 @@
         def _():
             partial(q)
 
-            @pl.when(t >= near_send.shape[0])
-            def _():
-                near_copy(q, t).wait_send()
-
             near_copy(q, t).start()
 
     def merge_near(q, t):
@@ -430,10 +452,11 @@
 
             @pl.when(jnp.logical_not(shared))
             def _():
-                @pl.when(layer > 0)
-                def _():
-                    for dz in range(1, layers):
-                        lone_copy(q, (layer + dz) % layers).start()
+                for at in range(1, layers):
+                    @pl.when(layer == at)
+                    def _():
+                        for z in relays(at):
+                            lone_copy(q, z).start()
 
                 last_copy(q).start()
 
@@ -471,37 +494,43 @@
                 def _():
                     far_copy(q, z).start()
 
-            @pl.when(jnp.logical_and(jnp.logical_not(shared), layer == 0))
-            def _():
-                for dz in reversed(range(1, layers)):
-                    diag_copy(q, dz).start()
+            for at in range(layers - 1):
+                straight = [z for z in reversed(range(at + 1, layers)) if not relayed(z, at)]
+                if straight:
+                    @pl.when(jnp.logical_and(jnp.logical_not(shared), layer == at))
+                    def _():
+                        for z in straight:
+                            diag_copy(q, z).start()
 
         @pl.when(jnp.logical_and(jnp.logical_not(held(q, chip)), jnp.logical_and(shared, layer > 0)))
         def _():
-            lone_come(q).wait_recv()
-            for dz in range(1, layers):
-                relay_copy(q, (layer + dz) % layers).start()
+            for lower in range(1, layers):
+                @pl.when(layer == lower)
+                def _():
+                    lone_part(q, len(relays(lower))).wait_recv()
+                    for z in relays(lower):
+                        relay_copy(q, z).start()
 
     def unit_at(t):
         turn = n // 2
         block_at, place = t // turn, t % turn
         early = jnp.where(place == turn - 1, both + block_at, block_at * (turn - 1) + place)
-        return jnp.where(layer == 0, early, t)
+        late = jnp.where(t < both + 2, t - 2, t)
+        return jnp.where(layer == 0, jnp.where(t < 2 * turn, early, late), t)
 
     def finish(c):
         near_part = held(c * cut, chip)
 
+        pieces = jnp.where(held(c * cut, across // 2), 1, 0)
         for dz in range(1, layers):
             source = (layer + dz) % layers
             passed = jnp.logical_and(source + 1 < layer, held(c * cut, 2 * (source + 1) + side))
-
-            @pl.when(jnp.logical_and(held(c * cut, 2 * source), jnp.logical_not(passed)))
-            def _():
-                far_come(c, source, dz).wait_recv()
-
-        @pl.when(held(c * cut, across // 2))
-        def _():
-            last_come(c).wait_recv()
+            sends = jnp.logical_and(held(c * cut, 2 * source), jnp.logical_not(passed))
+            pieces = pieces + jnp.where(sends, 1, 0)
+        for number in range(1, layers + 1):
+            @pl.when(pieces == number)
+            def _():
+                come(c, number).wait_recv()
 
         for half in range(cut):
             q = c * cut + half
@@ -529,10 +558,11 @@
 
     temps_ref[...] = jnp.zeros(temps_ref.shape, F32)
     basis_copy.wait()
+    early = jnp.logical_and(layer == 1, side == 0)
 
     def out_copy(step):
         at = pl.ds(step * FINE, FINE)
-        return pltpu.make_async_copy(temps_ref.at[at, :], out_hbm.at[at, :], out_sem.at[step])
+        return pltpu.make_async_copy(temps_ref.at[at, :], out_hbm.at[at, :], out_sem)
 
     def stage(tile, after=None):
         @pl.loop((tile * lanes + own - 1) // own, ((tile + 1) * lanes + own - 1) // own)
@@ -567,11 +597,13 @@
             def _(q):
                 last_copy(q).start()
 
+        @pl.when(jnp.logical_and(early, t == mine + 1))
+        def _():
+            stage(0)
+
         @pl.when(t >= lag)
         def _():
             pass_on(unit_at(t - lag), t - lag)
-
-    ring = near_send.shape[0]
 
     @pl.loop(0, n)
     def _(target):
@@ -579,13 +611,12 @@
         def _():
             seed_copy(me, target).wait_send()
 
-    @pl.loop(0, ring)
-    def _(k):
-        @pl.when(held(unit_at(k), chip))
-        def _():
-            near_copy(k, k).wait_send()
-
-    @pl.loop(0, tiles - 1)
+    for k in range(2):
+        @pl.when(jnp.logical_and(layer > 0, spot(layer, 1 - side, k) + spot(0, side, core) < n))
+        def _():
+            hold_pass(k).wait_send()
+
+    @pl.loop(jnp.where(early, 1, 0), tiles - 1)
     def _(tile):
         stage(tile)
 
@@ -597,22 +628,28 @@
 
         @pl.when(chip == place)
         def _():
+            near = near_ref.at[pl.ds(0, count)]
+            remote(near, near, near_send, near_recv.at[0], across).wait_send()
             side = side_ref.at[pl.ds(0, pair), pl.ds(0, layers - 1)]
             remote(side, side, side_send.at[0], side_recv.at[0], across).wait_send()
             last = side_ref.at[pl.ds(0, count), 0]
-            remote(last, last, last_send.at[0], last_recv.at[0], across).wait_send()
+            remote(last, last, last_send.at[0], come_recv.at[0], across).wait_send()
             far = far_ref.at[pl.ds(0, layers - 1), pl.ds(0, count)]
-            remote(far, far, far_send.at[0], far_recv.at[0, 0], across).wait_send()
-
-    sends_lone = jnp.logical_or(side == 0, layer > 0)
-
-    @pl.when(sends_lone)
-    def _():
-        for k in range(lone_send.shape[0]):
-            remote(rest_of(side_ref.at[0]), rest_of(side_ref.at[0]), lone_send.at[k], lone_recv.at[k], across).wait_send()
-
-    for step in range(out_sem.shape[0]):
-        out_copy(step).wait()
+            remote(far, far, far_send.at[0], come_recv.at[0], across).wait_send()
+
+    for lower in range(layers):
+        @pl.when(jnp.logical_and(layer == lower, side == 0))
+        def _():
+            for k in range(lone_send.shape[0]):
+                lone_part(both + k, layers - 1).wait_send()
+
+        if lower:
+            @pl.when(jnp.logical_and(layer == lower, side == 1))
+            def _():
+                for k in range(lone_send.shape[0]):
+                    lone_part(both + k, len(relays(lower))).wait_send()
+
+    pltpu.make_async_copy(temps_ref, out_hbm, out_sem).wait()
 
 
 def exchanged_temps(coefficients, legendre, row_counts, basis, n, points):
@@ -647,6 +684,7 @@
             pltpu.VMEM((n * block, LANES), F32),
             pltpu.VMEM((n, block, LANES), F32),
             pltpu.VMEM((n, block, LANES), F32),
+            pltpu.VMEM((2, block, LANES), F32),
             pltpu.VMEM((room * 2 * slots, LANES), F32),
             pltpu.VMEM((units, 2, 2, layers, width, columns), F32),
             pltpu.VMEM((units, 2, layers, width, columns), F32),
@@ -658,11 +696,11 @@
             pltpu.VMEM((FINE, LANES), F32),
             pltpu.VMEM((waves // LANES, points, 2 * LANES), BF16),
             pltpu.VMEM((waves // LANES, points, 2 * LANES), BF16),
-            dma((n // 2,)), dma, dma, dma((points // FINE,)), dma((n,)), dma((n,)),
-            dma((8,)), dma((8,)),
+            dma((n // 2,)), dma, dma, dma, dma((n,)), dma((n,)), dma((2,)), dma((2,)),
+            dma, dma((8,)),
             dma((1,)), dma((16,)),
             dma((1,)), dma((n,)),
-            dma((1,)), dma((layers - 1, n)), dma((units - 4 * cut,)), dma((2 * cut,)), dma((2 * cut,)),
+            dma((1,)), dma((units - 4 * cut,)), dma((2 * cut,)), dma((2 * cut,)),
         ],
         compiler_params=pltpu.CompilerParams(
             collective_id=0, has_side_effects=True, vmem_limit_bytes=58 * 1024 * 1024

time: 71.2 us -> 70.5 us (level)
  no operation moved by 1% of the time
where the time goes in v5:
time: 70.5 us; the launch traced here: 70.2 us
  Pallas kernels  69.5 us (99%)
    pallas_call x1, Pallas kernels, exchanged_temps(): pl.pallas_call(body, out_shape=jax.ShapeDtypeStruct((points, 2 * basis.sh...  63.8 us
    pallas_call x1, Pallas kernels, radiate_row(): pl.pallas_call(row_kernel, out_shape=jax.ShapeDtypeStruct((1, 2, points,...  5.71 us

profile of v5, /device:TPU:12, one launch (start us, length us, event | category | flops | bytes accessed | tf_op | source)
XLA Modules:
  0.0 70.2 jit_solution(6715840670752768685)
XLA Ops:
  0.7 63.8 %exchanged_temps.1.temps_ref = f32[1280,256]{1,0:T(8,128)} custom-call(s32[1]{0:T(128)S(6)} %copy.8.refs_0_.count_ref, bf16[25600,128]{1,0:T(8,128)(2,1)} %bitcast.9, f32[1280,320]{1,0:T(8,128)} %bitcast.10, f32[64,128]{1,0:T(8,128)} %refs_3_.1), custom_call_target="tpu_custom_call" | custom-call | tf_op jit(solution)/shard_map/exchanged_temps/pallas_call | solution.py:673
  64.5 5.7 %row_radiance.1 = f32[1,2,1280,512]{3,2,1,0:T(8,128)} custom-call(s32[1]{0:T(128)S(6)} %copy.8.refs_0_.count_ref, f32[1280,256]{1,0:T(8,128)} %exchanged_temps.1.temps_ref, f32[1,128]{1,0:T(1,128)} %bitcast.13, s32[1,512]{1,0:T(1,128)} %bitcast.11, f32[1,512]{1,0:T(1,128)} %bitcast.12), custom_call_target="tpu_custom_call" | custom-call | tf_op jit(solution)/shard_map/row_radiance/pallas_call | solution.py:775

commit v6 on v5

--- a/solution.py
+++ b/solution.py
@@ -138,11 +138,11 @@
         )
 
     def seed_copy(source, target):
-        return remote(send_ref.at[target], seed_ref.at[source], seed_send.at[target], seed_recv.at[source], target)
+        return remote(send_ref.at[target], seed_ref.at[source], seed_send, seed_recv.at[source], target)
 
     def hold_copy(place, target):
         at = spot(layer, 1 - side, place)
-        return remote(send_ref.at[target], hold_ref.at[core], seed_send.at[target], hold_recv.at[core], at)
+        return remote(send_ref.at[target], hold_ref.at[core], seed_send, hold_recv.at[core], at)
 
     def hold_come(k):
         return remote(hold_ref.at[k], hold_ref.at[k], hold_send.at[k], hold_recv.at[k], across)
@@ -253,6 +253,16 @@
     basis_copy = pltpu.make_async_copy(basis_hbm, basis_ref, basis_sem)
     basis_copy.start()
 
+    def greet():
+        pl.semaphore_wait(barrier, len(corners) - 1)
+        for dz in range(1, layers):
+            for offset in corners:
+                signal(corner(dz, offset))
+
+    @pl.when(jnp.logical_and(layer == 0, side == 1))
+    def _():
+        greet()
+
     row = lax.broadcasted_iota(jnp.int32, (lanes, lanes), 0)
     lane = lax.broadcasted_iota(jnp.int32, (lanes, lanes), 1)
     row_at = row % rows
@@ -261,10 +271,7 @@
 
     raw_ref[...] = jnp.zeros(raw_ref.shape, F32)
     leg_copy.wait()
-    for q in range(pieces):
-        @pl.when(me + q * share < n)
-        def _():
-            coef_copy(q).start()
+    coef_copy(0).start()
 
     for g in range(cut * groups):
         at = (g // groups) * 2 * room + g % groups
@@ -298,12 +305,12 @@
         def _():
             seed_copy(me, target).start()
 
+    @pl.when(jnp.logical_and(layer == 0, side == 0))
+    def _():
+        greet()
+
     @pl.when(layer == 0)
     def _():
-        pl.semaphore_wait(barrier, len(corners) - 1)
-        for dz in range(1, layers):
-            for offset in corners:
-                signal(corner(dz, offset))
         for offset in corners[1:]:
             give_seeds(layer, offset)
 
@@ -332,6 +339,11 @@
             def _():
                 hold_come(k).wait_recv()
                 hold_pass(k).start()
+
+    for q in range(1, pieces):
+        @pl.when(me + q * share < n)
+        def _():
+            coef_copy(q).start()
 
     tiles = waves // lanes
 
@@ -564,16 +576,49 @@
         at = pl.ds(step * FINE, FINE)
         return pltpu.make_async_copy(temps_ref.at[at, :], out_hbm.at[at, :], out_sem)
 
+    def drain():
+        for place in range(n // 2):
+            count = cut * (n - 2 * place)
+            pair = cut * (n - 2 * (place // 2 * 2 + 1))
+
+            @pl.when(chip == place)
+            def _():
+                near = near_ref.at[pl.ds(0, count)]
+                remote(near, near, near_send, near_recv.at[0], across).wait_send()
+                side = side_ref.at[pl.ds(0, pair), pl.ds(0, layers - 1)]
+                remote(side, side, side_send.at[0], side_recv.at[0], across).wait_send()
+                last = side_ref.at[pl.ds(0, count), 0]
+                remote(last, last, last_send.at[0], come_recv.at[0], across).wait_send()
+                far = far_ref.at[pl.ds(0, layers - 1), pl.ds(0, count)]
+                remote(far, far, far_send.at[0], come_recv.at[0], across).wait_send()
+
+        for lower in range(layers):
+            @pl.when(jnp.logical_and(layer == lower, side == 0))
+            def _():
+                for k in range(lone_send.shape[0]):
+                    lone_part(both + k, layers - 1).wait_send()
+
+            if lower:
+                @pl.when(jnp.logical_and(layer == lower, side == 1))
+                def _():
+                    for k in range(lone_send.shape[0]):
+                        lone_part(both + k, len(relays(lower))).wait_send()
+
     def stage(tile, after=None):
         @pl.loop((tile * lanes + own - 1) // own, ((tile + 1) * lanes + own - 1) // own)
         def _(c):
             finish(c)
 
+        if after is not None:
+            @pl.when(layer > 0)
+            def _():
+                drain()
+
         add_tile(tile, spectra_ref, basis_ref, high_ref, low_ref, temps_ref, after)
 
     @pl.loop(0, units + lag)
     def _(t):
-        @pl.when(t == lag)
+        @pl.when(t == lag - 1)
         def _():
             meet()
 
@@ -605,11 +650,11 @@
         def _():
             pass_on(unit_at(t - lag), t - lag)
 
-    @pl.loop(0, n)
-    def _(target):
-        @pl.when(jnp.logical_and(target != me, me + target < n))
-        def _():
-            seed_copy(me, target).wait_send()
+    for number in range(1, n):
+        @pl.when(jnp.where(2 * me < n, n - me - 1, n - me) == number)
+        def _():
+            gone = send_ref.at[pl.ds(0, number)]
+            remote(gone, gone, seed_send, seed_recv.at[0], across).wait_send()
 
     for k in range(2):
         @pl.when(jnp.logical_and(layer > 0, spot(layer, 1 - side, k) + spot(0, side, core) < n))
@@ -622,32 +667,9 @@
 
     stage(tiles - 1, lambda step: out_copy(step).start())
 
-    for place in range(n // 2):
-        count = cut * (n - 2 * place)
-        pair = cut * (n - 2 * (place // 2 * 2 + 1))
-
-        @pl.when(chip == place)
-        def _():
-            near = near_ref.at[pl.ds(0, count)]
-            remote(near, near, near_send, near_recv.at[0], across).wait_send()
-            side = side_ref.at[pl.ds(0, pair), pl.ds(0, layers - 1)]
-            remote(side, side, side_send.at[0], side_recv.at[0], across).wait_send()
-            last = side_ref.at[pl.ds(0, count), 0]
-            remote(last, last, last_send.at[0], come_recv.at[0], across).wait_send()
-            far = far_ref.at[pl.ds(0, layers - 1), pl.ds(0, count)]
-            remote(far, far, far_send.at[0], come_recv.at[0], across).wait_send()
-
-    for lower in range(layers):
-        @pl.when(jnp.logical_and(layer == lower, side == 0))
-        def _():
-            for k in range(lone_send.shape[0]):
-                lone_part(both + k, layers - 1).wait_send()
-
-        if lower:
-            @pl.when(jnp.logical_and(layer == lower, side == 1))
-            def _():
-                for k in range(lone_send.shape[0]):
-                    lone_part(both + k, len(relays(lower))).wait_send()
+    @pl.when(layer == 0)
+    def _():
+        drain()
 
     pltpu.make_async_copy(temps_ref, out_hbm, out_sem).wait()
 
@@ -696,9 +718,9 @@
             pltpu.VMEM((FINE, LANES), F32),
             pltpu.VMEM((waves // LANES, points, 2 * LANES), BF16),
             pltpu.VMEM((waves // LANES, points, 2 * LANES), BF16),
-            dma((n // 2,)), dma, dma, dma, dma((n,)), dma((n,)), dma((2,)), dma((2,)),
+            dma((n // 2,)), dma, dma, dma, dma, dma((n,)), dma((2,)), dma((2,)),
             dma, dma((8,)),
-            dma((1,)), dma((16,)),
+            dma((1,)), dma((12,)),
             dma((1,)), dma((n,)),
             dma((1,)), dma((units - 4 * cut,)), dma((2 * cut,)), dma((2 * cut,)),
         ],

time: 70.5 us -> 70.1 us (level)
  no operation moved by 1% of the time
where the time goes in v6:
time: 70.1 us; the launch traced here: 69.9 us
  Pallas kernels  69.3 us (99%)
    pallas_call x1, Pallas kernels, exchanged_temps(): pl.pallas_call(body, out_shape=jax.ShapeDtypeStruct((points, 2 * basis.sh...  63.6 us
    pallas_call x1, Pallas kernels, radiate_row(): pl.pallas_call(row_kernel, out_shape=jax.ShapeDtypeStruct((1, 2, points,...  5.71 us

profile of v6, /device:TPU:12, one launch (start us, length us, event | category | flops | bytes accessed | tf_op | source)
XLA Modules:
  0.0 69.9 jit_solution(17317799847873127363)
XLA Ops:
  0.7 63.6 %exchanged_temps.1.temps_ref = f32[1280,256]{1,0:T(8,128)} custom-call(s32[1]{0:T(128)S(6)} %copy.8.refs_0_.count_ref, bf16[25600,128]{1,0:T(8,128)(2,1)} %bitcast.9, f32[1280,320]{1,0:T(8,128)} %bitcast.10, f32[64,128]{1,0:T(8,128)} %refs_3_.1), custom_call_target="tpu_custom_call" | custom-call | tf_op jit(solution)/shard_map/exchanged_temps/pallas_call | solution.py:695
  64.2 5.7 %row_radiance.1 = f32[1,2,1280,512]{3,2,1,0:T(8,128)} custom-call(s32[1]{0:T(128)S(6)} %copy.8.refs_0_.count_ref, f32[1280,256]{1,0:T(8,128)} %exchanged_temps.1.temps_ref, f32[1,128]{1,0:T(1,128)} %bitcast.13, s32[1,512]{1,0:T(1,128)} %bitcast.11, f32[1,512]{1,0:T(1,128)} %bitcast.12), custom_call_target="tpu_custom_call" | custom-call | tf_op jit(solution)/shard_map/row_radiance/pallas_call | solution.py:797

commit v7 on v6

--- a/solution.py
+++ b/solution.py
@@ -10,6 +10,7 @@
 NLON = 1280
 FINE = 256
 SPAN = 640
+PARTS = 4
 LANES = 128
 
 PRECISE = lax.Precision.HIGHEST
@@ -751,67 +752,77 @@
     )(row_counts, spectra, basis)
 
 
-def row_kernel(count_ref, temps_ref, absorb_ref, peak_ref, width_ref, out_ref, rhigh_ref, rlow_ref):
-    step = pl.program_id(0)
+def row_kernel(
+    count_ref, temps_hbm, absorb_ref, peak_ref, width_ref, out_hbm, temps_ref, out_ref, pair_ref, rhigh_ref, rlow_ref,
+    temps_sem, out_sem,
+):
     levels = absorb_ref.shape[1]
     points = temps_ref.shape[0]
-
-    @pl.when(step == 0)
-    def _():
-        height = lax.broadcasted_iota(jnp.int32, rlow_ref.shape, 0)
-        offsets = (height - peak_ref[...]).astype(F32) / width_ref[...]
-        shape = jnp.exp(-offsets * offsets)
-        high, low = split(shape / jnp.sum(shape, axis=0, keepdims=True))
-        rhigh_ref[pl.ds(0, levels), :] = high
-        rhigh_ref[pl.ds(levels, levels), :] = high
-        rlow_ref[...] = low
-
-    temps = temps_ref[...]
-    temps = jnp.concatenate((temps[:, :levels], temps[:, levels:]), axis=0)
-
-    source = jnp.exp(0.5 * temps)
-    layers = absorb_ref[...] * source
-    before = lax.broadcasted_iota(jnp.int32, (2 * levels, levels), 0) % levels
-    after = lax.broadcasted_iota(jnp.int32, (2 * levels, levels), 1)
-    upper = jnp.where(before < after, 1.0, 0.0).astype(BF16)
-    layers_high, layers_low = split(layers)
-    above = dot(jnp.concatenate((layers_high, layers_low), axis=1), upper)
-    emitted = source * jnp.exp(-above) * (1.0 - jnp.exp(-layers))
-    place = step * points + lax.broadcasted_iota(jnp.int32, (2 * points, levels), 0) % points
-    emitted = jnp.where(place < count_ref[0], emitted, 0.0)
-    emitted_high, emitted_low = split(emitted)
-    bright = dot(jnp.concatenate((emitted_high, emitted_low), axis=1), rhigh_ref[...])
-    bright = bright + dot(emitted_high, rlow_ref[...])
-    out_ref[0, 0] = bright[:points]
-    out_ref[0, 1] = bright[points:]
+    chunk = pair_ref.shape[0] // 2
+    steps = points // chunk
+    piece = chunk // PARTS
+
+    def come(step):
+        at = pl.ds(pl.multiple_of(step * chunk, chunk), chunk)
+        return pltpu.make_async_copy(temps_hbm.at[at, :], temps_ref.at[at, :], temps_sem.at[step])
+
+    for step in range(steps):
+        come(step).start()
+    height = lax.broadcasted_iota(jnp.int32, rlow_ref.shape, 0)
+    offsets = (height - peak_ref[...]).astype(F32) / width_ref[...]
+    shape = jnp.exp(-offsets * offsets)
+    high, low = split(shape / jnp.sum(shape, axis=0, keepdims=True))
+    rhigh_ref[pl.ds(0, levels), :] = high
+    rhigh_ref[pl.ds(levels, levels), :] = high
+    rlow_ref[...] = low
+
+    @pl.loop(0, steps)
+    def _(step):
+        come(step).wait()
+        first = pl.multiple_of(step * chunk, chunk)
+        temps = temps_ref[pl.ds(first, chunk), :]
+        temps = jnp.concatenate((temps[:, :levels], temps[:, levels:]), axis=0)
+        source = jnp.exp(0.5 * temps)
+        layers = absorb_ref[...] * source
+        before = lax.broadcasted_iota(jnp.int32, (2 * levels, levels), 0) % levels
+        after = lax.broadcasted_iota(jnp.int32, (2 * levels, levels), 1)
+        upper = jnp.where(before < after, 1.0, 0.0).astype(BF16)
+        layers_high, layers_low = split(layers)
+        above = dot(jnp.concatenate((layers_high, layers_low), axis=1), upper)
+        emitted = source * jnp.exp(-above) * (1.0 - jnp.exp(-layers))
+        place = first + lax.broadcasted_iota(jnp.int32, (2 * chunk, levels), 0) % chunk
+        emitted = jnp.where(place < count_ref[0], emitted, 0.0)
+        pair_ref[...] = jnp.concatenate(split(emitted), axis=1)
+        for half in range(2):
+            for part in range(PARTS):
+                pair = pair_ref[pl.ds(half * chunk + part * piece, piece), :]
+                bright = dot(pair, rhigh_ref[...]) + dot(pair[:, :levels], rlow_ref[...])
+                at = pl.ds(pl.multiple_of(first + part * piece, piece), piece)
+                out_ref[0, half, at, :] = bright
+                pltpu.make_async_copy(out_ref.at[0, half, at, :], out_hbm.at[0, half, at, :], out_sem).start()
+
+    pltpu.make_async_copy(out_ref, out_hbm, out_sem).wait()
 
 
 def radiate_row(temps, row_counts, absorb, peak_level, width):
     points = temps.shape[0]
+    levels, channels = absorb.shape[0], width.shape[0]
     span = SPAN if points % SPAN == 0 else FINE
-    levels, channels = absorb.shape[0], width.shape[0]
-
-    def whole(*shape):
-        return pl.BlockSpec(shape, lambda i, *_: (0,) * len(shape))
-
+    vmem = pl.BlockSpec(memory_space=pltpu.VMEM)
     return pl.pallas_call(
         row_kernel,
         out_shape=jax.ShapeDtypeStruct((1, 2, points, channels), F32),
-        grid_spec=pltpu.PrefetchScalarGridSpec(
-            num_scalar_prefetch=1,
-            grid=(points // span,),
-            in_specs=[
-                pl.BlockSpec((span, 2 * levels), lambda i, *_: (i, 0)),
-                whole(1, levels),
-                whole(1, channels),
-                whole(1, channels),
-            ],
-            out_specs=pl.BlockSpec((1, 2, span, channels), lambda i, *_: (0, 0, i, 0)),
-            scratch_shapes=[
-                pltpu.VMEM((2 * levels, channels), BF16),
-                pltpu.VMEM((levels, channels), BF16),
-            ],
-        ),
+        in_specs=[pl.BlockSpec(memory_space=pltpu.SMEM), pl.BlockSpec(memory_space=pl.ANY), vmem, vmem, vmem],
+        out_specs=pl.BlockSpec(memory_space=pl.ANY),
+        scratch_shapes=[
+            pltpu.VMEM(temps.shape, F32),
+            pltpu.VMEM((1, 2, points, channels), F32),
+            pltpu.VMEM((2 * span, 2 * levels), BF16),
+            pltpu.VMEM((2 * levels, channels), BF16),
+            pltpu.VMEM((levels, channels), BF16),
+            pltpu.SemaphoreType.DMA((points // span,)),
+            pltpu.SemaphoreType.DMA,
+        ],
         name="row_radiance",
     )(row_counts, temps, absorb[None, :], peak_level[None, :], width[None, :])
 

time: 70.1 us -> 69.5 us (level)
  no operation moved by 1% of the time
where the time goes in v7:
time: 69.5 us; the launch traced here: 69.3 us
  Pallas kernels  68.7 us (99%)
    pallas_call x1, Pallas kernels, exchanged_temps(): pl.pallas_call(body, out_shape=jax.ShapeDtypeStruct((points, 2 * basis.sh...  63.6 us
    pallas_call x1, Pallas kernels, radiate_row(): pl.pallas_call(row_kernel, out_shape=jax.ShapeDtypeStruct((1, 2, points,...  5.11 us

profile of v7, /device:TPU:12, one launch (start us, length us, event | category | flops | bytes accessed | tf_op | source)
XLA Modules:
  0.0 69.3 jit_solution(8243988236595286580)
XLA Ops:
  0.7 63.6 %exchanged_temps.1.temps_hbm = f32[1280,256]{1,0:T(8,128)} custom-call(s32[1]{0:T(128)S(6)} %copy.8.refs_0_.count_ref, bf16[25600,128]{1,0:T(8,128)(2,1)} %bitcast.9, f32[1280,320]{1,0:T(8,128)} %bitcast.10, f32[64,128]{1,0:T(8,128)} %refs_3_.1), custom_call_target="tpu_custom_call" | custom-call | tf_op jit(solution)/shard_map/exchanged_temps/pallas_call | solution.py:696
  64.2 5.1 %row_radiance.1 = f32[1,2,1280,512]{3,2,1,0:T(8,128)} custom-call(s32[1]{0:T(128)S(6)} %copy.8.refs_0_.count_ref, f32[1280,256]{1,0:T(8,128)} %exchanged_temps.1.temps_hbm, f32[1,128]{1,0:T(1,128)} %bitcast.13, s32[1,512]{1,0:T(1,128)} %bitcast.11, f32[1,512]{1,0:T(1,128)} %bitcast.12), custom_call_target="tpu_custom_call" | custom-call | tf_op jit(solution)/shard_map/row_radiance/pallas_call | solution.py:812

commit v8 on v7

--- a/solution.py
+++ b/solution.py
@@ -127,7 +127,7 @@
     across = me + 2 - 4 * side
     both = cut * (n - 2 * (2 * layer + 1))
     mine = cut * (n - 4 * layer)
-    lag = 5
+    lag = 6
 
     def spot(z, y, c):
         return (z * 2 + y) * 2 + c
@@ -619,7 +619,7 @@
 
     @pl.loop(0, units + lag)
     def _(t):
-        @pl.when(t == lag - 1)
+        @pl.when(t == lag - 2)
         def _():
             meet()
 
@@ -721,7 +721,7 @@
             pltpu.VMEM((waves // LANES, points, 2 * LANES), BF16),
             dma((n // 2,)), dma, dma, dma, dma, dma((n,)), dma((2,)), dma((2,)),
             dma, dma((8,)),
-            dma((1,)), dma((12,)),
+            dma((1,)), dma((16,)),
             dma((1,)), dma((n,)),
             dma((1,)), dma((units - 4 * cut,)), dma((2 * cut,)), dma((2 * cut,)),
         ],

time: 69.5 us -> 69.1 us (level)
  no operation moved by 1% of the time
where the time goes in v8:
time: 69.1 us; the launch traced here: 68.8 us
  Pallas kernels  68.2 us (99%)
    pallas_call x1, Pallas kernels, exchanged_temps(): pl.pallas_call(body, out_shape=jax.ShapeDtypeStruct((points, 2 * basis.sh...  63.1 us
    pallas_call x1, Pallas kernels, radiate_row(): pl.pallas_call(row_kernel, out_shape=jax.ShapeDtypeStruct((1, 2, points,...  5.11 us

profile of v8, /device:TPU:12, one launch (start us, length us, event | category | flops | bytes accessed | tf_op | source)
XLA Modules:
  0.0 68.8 jit_solution(3247069299356912841)
XLA Ops:
  0.7 63.1 %exchanged_temps.1.temps_hbm = f32[1280,256]{1,0:T(8,128)} custom-call(s32[1]{0:T(128)S(6)} %copy.8.refs_0_.count_ref, bf16[25600,128]{1,0:T(8,128)(2,1)} %bitcast.9, f32[1280,320]{1,0:T(8,128)} %bitcast.10, f32[64,128]{1,0:T(8,128)} %refs_3_.1), custom_call_target="tpu_custom_call" | custom-call | tf_op jit(solution)/shard_map/exchanged_temps/pallas_call | solution.py:696
  63.7 5.1 %row_radiance.1 = f32[1,2,1280,512]{3,2,1,0:T(8,128)} custom-call(s32[1]{0:T(128)S(6)} %copy.8.refs_0_.count_ref, f32[1280,256]{1,0:T(8,128)} %exchanged_temps.1.temps_hbm, f32[1,128]{1,0:T(1,128)} %bitcast.13, s32[1,512]{1,0:T(1,128)} %bitcast.11, f32[1,512]{1,0:T(1,128)} %bitcast.12), custom_call_target="tpu_custom_call" | custom-call | tf_op jit(solution)/shard_map/row_radiance/pallas_call | solution.py:812
